TPU v7x, 32 devices: a whole 2x2x4 slice. The times are simulated.
32 devices in a mesh: groups: 2 (over x), seq: 16 (over z, y, core).
Axes of the slice: x: 2, y: 2, z: 4, core: 2. Of those that a mesh axis runs over, the one named last changes fastest.
Arguments:
- queries: bfloat16 [8192, 768], P(('groups', 'seq')), parts along dimension 0, may hold values from -6 to 6
- keys_values: bfloat16 [2, 8192, 768], P(None, ('groups', 'seq')), parts along dimension 1, may hold values from -6 to 6
- cotangent: bfloat16 [8192, 768], P(('groups', 'seq')), parts along dimension 0, may hold values from -6 to 6
- frame_lists: int32 [64, 6], P(('groups', 'seq')), parts along dimension 0, may hold values from 0 to 15
- sink_owner: int32 [2], P('groups'), parts along dimension 0, may hold values from 0 to 15
Outputs:
- attended: bfloat16 [8192, 768], P(('groups', 'seq')), parts along dimension 0
- grad_queries: bfloat16 [8192, 768], P(('groups', 'seq')), parts along dimension 0
- grad_keys_values: bfloat16 [2, 8192, 768], P(None, ('groups', 'seq')), parts along dimension 1
There are 2 independent parts, one for each index of `groups`. A program takes and returns all parts, laid end to end along the dimension named above; each array names one. Nothing has to cross between parts.
Inputs may be any that keep to these rules, and one draw needn't show every extreme that they name: `frame_lists`: entries may repeat within a row.
All inputs are finite; a program needn't handle non-finite values.
Results may differ from a plain program's by a relative error of at most 0.025.
Values may be sent and summed in bfloat16 or wider, within the bound.
A program may use at most 128 MiB of HBM per device.

v0:
```python
from functools import partial
import math

import jax
import jax.numpy as jnp
from jax import lax
from jax.sharding import PartitionSpec as P

HEAD = 64
BLK = 128


def spread(shard, axis, root):
    mine = lax.axis_index(axis) == root
    return lax.psum(jnp.where(mine, shard, jnp.zeros_like(shard)), axis)


def anchor_span(device_ids, axis_length):
    return jnp.where(device_ids % 2 == 0, device_ids, 2 * axis_length - 1 - device_ids)


def build_masks(frame_ids, span_index, sink_device, axis_length, row_count):
    block_count, entry_count = frame_ids.shape
    entry_order = jnp.arange(entry_count)
    repeated = jnp.any(
        (frame_ids[:, :, None] == frame_ids[:, None, :])
        & (entry_order[None, None, :] < entry_order[None, :, None]),
        axis=2,
    )
    is_valid = (
        (anchor_span(frame_ids, axis_length) < span_index)
        & (frame_ids != sink_device)
        & jnp.logical_not(repeated)
    )
    key_valid = jnp.repeat(jnp.repeat(is_valid, BLK, axis=1), row_count // block_count, axis=0)
    position = jnp.arange(row_count)
    in_sink = (span_index == anchor_span(sink_device, axis_length)) & (position < BLK)
    window = (position[None, :] <= position[:, None]) & jnp.logical_not(in_sink[None, :])
    return (window, key_valid)


def tier_products(left_rows, right_rows, picked_right, sink_right):
    row_count = left_rows.shape[0]
    block_count = picked_right.shape[0]
    left_heads = left_rows.reshape(row_count, -1, HEAD)
    window_part = jnp.einsum(
        "qhd,khd->hqk",
        left_heads,
        right_rows.reshape(row_count, -1, HEAD),
        preferred_element_type=jnp.float32,
    )
    sink_part = jnp.einsum(
        "qhd,khd->hqk",
        left_heads,
        sink_right.reshape(BLK, -1, HEAD),
        preferred_element_type=jnp.float32,
    )
    left_blocks = left_rows.reshape(block_count, row_count // block_count, -1, HEAD)
    right_blocks = picked_right.reshape(block_count, picked_right.shape[1], -1, HEAD)
    anchor_part = jnp.einsum(
        "bqhd,bkhd->hbqk", left_blocks, right_blocks, preferred_element_type=jnp.float32
    )
    return (window_part, sink_part, anchor_part.reshape(left_heads.shape[1], row_count, -1))


def tier_scores(query_rows, key_rows, picked_keys, sink_keys, window, key_valid):
    score_scale = 1.0 / math.sqrt(HEAD)
    window_part, sink_part, anchor_part = tier_products(
        query_rows, key_rows, picked_keys, sink_keys
    )
    window_part = jnp.where(window[None], window_part * score_scale, -jnp.inf)
    anchor_part = jnp.where(key_valid[None], anchor_part * score_scale, -jnp.inf)
    return (window_part, sink_part * score_scale, anchor_part)


def normalized(scores):
    window_part, sink_part, anchor_part = scores
    row_max = jnp.maximum(
        jnp.maximum(jnp.max(window_part, axis=-1), jnp.max(sink_part, axis=-1)),
        jnp.max(anchor_part, axis=-1),
    )
    summed = jnp.sum(jnp.exp(window_part - row_max[..., None]), axis=-1)
    summed = summed + jnp.sum(jnp.exp(sink_part - row_max[..., None]), axis=-1)
    summed = summed + jnp.sum(jnp.exp(anchor_part - row_max[..., None]), axis=-1)
    log_total = row_max + jnp.log(summed)
    return (
        jnp.exp(window_part - log_total[..., None]),
        jnp.exp(sink_part - log_total[..., None]),
        jnp.exp(anchor_part - log_total[..., None]),
    )


def lowered(weights):
    return (
        weights[0].astype(jnp.bfloat16),
        weights[1].astype(jnp.bfloat16),
        weights[2].astype(jnp.bfloat16),
    )


def attend(weights, window_rows, picked_rows, sink_rows):
    head_count, row_count = (weights[0].shape[0], weights[0].shape[1])
    block_count = picked_rows.shape[0]
    summed = jnp.einsum(
        "hqk,khd->qhd",
        weights[0],
        window_rows.reshape(row_count, -1, HEAD),
        preferred_element_type=jnp.float32,
    )
    summed = summed + jnp.einsum(
        "hqk,khd->qhd",
        weights[1],
        sink_rows.reshape(BLK, -1, HEAD),
        preferred_element_type=jnp.float32,
    )
    anchor_weights = weights[2].reshape(head_count, block_count, row_count // block_count, -1)
    anchor_part = jnp.einsum(
        "hbqk,bkhd->bqhd",
        anchor_weights,
        picked_rows.reshape(block_count, picked_rows.shape[1], -1, HEAD),
        preferred_element_type=jnp.float32,
    )
    return (summed + anchor_part.reshape(row_count, head_count, HEAD)).reshape(row_count, -1)


def key_side(weights, left_rows, block_count):
    head_count, row_count = (weights[0].shape[0], weights[0].shape[1])
    model_width = left_rows.shape[1]
    left_heads = left_rows.reshape(row_count, -1, HEAD)
    window_part = jnp.einsum(
        "hqk,qhd->khd", weights[0], left_heads, preferred_element_type=jnp.float32
    ).reshape(row_count, model_width)
    sink_part = jnp.einsum(
        "hqk,qhd->khd", weights[1], left_heads, preferred_element_type=jnp.float32
    ).reshape(BLK, model_width)
    anchor_weights = weights[2].reshape(head_count, block_count, row_count // block_count, -1)
    left_blocks = left_rows.reshape(block_count, row_count // block_count, -1, HEAD)
    anchor_part = jnp.einsum(
        "hbqk,bqhd->bkhd", anchor_weights, left_blocks, preferred_element_type=jnp.float32
    ).reshape(-1, BLK, model_width)
    return (window_part, sink_part, anchor_part)


def forward_span(
    query_rows,
    key_rows,
    value_rows,
    picked_keys,
    picked_values,
    window,
    key_valid,
    sink_keys,
    sink_values,
):
    weights = normalized(
        tier_scores(query_rows, key_rows, picked_keys, sink_keys, window, key_valid)
    )
    return attend(lowered(weights), value_rows, picked_values, sink_values).astype(jnp.bfloat16)


def backward_span(
    query_rows,
    key_rows,
    value_rows,
    grad_rows,
    attended_rows,
    picked_keys,
    picked_values,
    window,
    key_valid,
    sink_keys,
    sink_values,
):
    row_count = query_rows.shape[0]
    block_count = picked_keys.shape[0]
    score_scale = 1.0 / math.sqrt(HEAD)
    weights = normalized(
        tier_scores(query_rows, key_rows, picked_keys, sink_keys, window, key_valid)
    )
    weights_low = lowered(weights)
    row_delta = jnp.sum(
        grad_rows.reshape(row_count, -1, HEAD).astype(jnp.float32)
        * attended_rows.reshape(row_count, -1, HEAD).astype(jnp.float32),
        axis=-1,
    ).T[..., None]
    products = tier_products(grad_rows, value_rows, picked_values, sink_values)
    dscores = (
        (weights[0] * (products[0] - row_delta) * score_scale).astype(jnp.bfloat16),
        (weights[1] * (products[1] - row_delta) * score_scale).astype(jnp.bfloat16),
        (weights[2] * (products[2] - row_delta) * score_scale).astype(jnp.bfloat16),
    )
    grad_query = attend(dscores, key_rows, picked_keys, sink_keys)
    key_grads = key_side(dscores, query_rows, block_count)
    value_grads = key_side(weights_low, grad_rows, block_count)
    local_grads = jnp.stack((key_grads[0], value_grads[0]))
    entries = jnp.stack(
        (
            jnp.concatenate((key_grads[2], key_grads[1][None]), axis=0),
            jnp.concatenate((value_grads[2], value_grads[1][None]), axis=0),
        ),
        axis=1,
    )
    return (grad_query, local_grads, entries)


def pick_anchors(gathered, frame_slots):
    chosen = gathered[:, frame_slots]
    return chosen.reshape(2, frame_slots.shape[0], frame_slots.shape[1], -1, gathered.shape[3])


def shards(queries, keys_values, cotangent, frame_lists, sink_owner):
    axis_length = lax.axis_size("seq")
    device_index = lax.axis_index("seq")
    half_rows = queries.shape[0] // 2
    model_width = queries.shape[1]
    sink_device = sink_owner[0]
    anchor_offset = jnp.where(device_index % 2 == 0, 0, half_rows).astype(jnp.int32)
    own_anchor = lax.dynamic_slice_in_dim(keys_values, anchor_offset, BLK, axis=1)
    gathered = lax.all_gather(own_anchor, "seq", axis=1, tiled=True).reshape(
        2, axis_length, BLK, model_width
    )
    sink_pair = spread(own_anchor, "seq", sink_device)
    span_ids = jnp.stack((device_index, 2 * axis_length - 1 - device_index))
    frame_slots = frame_lists.reshape(2, -1, frame_lists.shape[1])
    masker = jax.vmap(
        partial(build_masks, axis_length=axis_length, row_count=half_rows), in_axes=(0, 0, None)
    )
    window, key_valid = masker(frame_slots, span_ids, sink_device)
    query_slots = queries.reshape(2, half_rows, model_width)
    key_slots = keys_values[0].reshape(2, half_rows, model_width)
    value_slots = keys_values[1].reshape(2, half_rows, model_width)
    grad_slots = cotangent.reshape(2, half_rows, model_width)
    picked = pick_anchors(gathered, frame_slots)
    forward = jax.vmap(forward_span, in_axes=(0, 0, 0, 0, 0, 0, 0, None, None))
    attended_slots = forward(
        query_slots,
        key_slots,
        value_slots,
        picked[0],
        picked[1],
        window,
        key_valid,
        sink_pair[0],
        sink_pair[1],
    )
    backward = jax.vmap(backward_span, in_axes=(0, 0, 0, 0, 0, 0, 0, 0, 0, None, None))
    grad_query, local_grads, entries = backward(
        query_slots,
        key_slots,
        value_slots,
        grad_slots,
        attended_slots,
        picked[0],
        picked[1],
        window,
        key_valid,
        sink_pair[0],
        sink_pair[1],
    )
    owner_ids = jnp.concatenate(
        (frame_slots.reshape(2, -1), jnp.broadcast_to(sink_device, (2, 1))), axis=1
    ).reshape(-1)
    flat_entries = entries.reshape(-1, 2, BLK, model_width)
    inside = (owner_ids >= 0) & (owner_ids < 1 * lax.axis_size("seq"))
    targets = jnp.where(inside, owner_ids, 1 * lax.axis_size("seq"))
    empty = jnp.zeros((1 * lax.axis_size("seq"), 2, BLK, model_width), jnp.float32)
    reduced = lax.psum_scatter(
        empty.at[targets].add(flat_entries, mode="drop").astype(jnp.bfloat16),
        "seq",
        scatter_dimension=0,
        tiled=True,
    ).astype(jnp.float32)[0]
    own_grads = local_grads.transpose(1, 0, 2, 3).reshape(2, 2 * half_rows, model_width)
    anchor_rows = lax.dynamic_slice_in_dim(own_grads, anchor_offset, BLK, axis=1) + reduced
    own_grads = lax.dynamic_update_slice_in_dim(own_grads, anchor_rows, anchor_offset, axis=1)
    attended = attended_slots.reshape(2 * half_rows, model_width)
    return (
        attended,
        grad_query.reshape(2 * half_rows, model_width).astype(jnp.bfloat16),
        own_grads.astype(jnp.bfloat16),
    )


def solution(mesh):
    return jax.shard_map(
        shards,
        mesh=mesh,
        in_specs=(
            P(("groups", "seq"), None),
            P(None, ("groups", "seq"), None),
            P(("groups", "seq"), None),
            P(("groups", "seq"), None),
            P("groups"),
        ),
        out_specs=(
            P(("groups", "seq"), None),
            P(("groups", "seq"), None),
            P(None, ("groups", "seq"), None),
        ),
        check_vma=False,
    )
```

profile of v0, /device:TPU:11, one launch (start us, length us, event | category | flops | bytes accessed | tf_op | source)
XLA Modules:
  0.0 407.0 jit_solution(11507056745562765799)
XLA Ops:
  7.9 1.9 broadcast_select_fusion
  12.4 1.0 and_reduce_fusion
  14.2 1.2 copy.192
  15.5 1.3 copy.209
  19.1 1.1 fusion.58
  20.2 81.2 %all-reduce.3.cloned.1.call-done = bf16[2,128,768]{2,1,0:T(8,128)(2,1)} async-done(((bf16[2,128,768]{2,1,0:T(8,128)(2,1)}), bf16[2,128,768]{2,1,0:T(8,128)(2,1)}) %all-reduce.3.cloned.1.call-update) | async-done | bytes 393232 | tf_op jit(solution)/shard_map/psum | solution.py:15
  101.4 1.0 fusion.57
  104.1 2.1 fusion.59
  106.2 61.7 %all-gather.2.cloned.1.call-done = bf16[2,2048,768]{2,1,0:T(8,128)(2,1)} async-done(((bf16[2,128,768]{2,1,0:T(8,128)(2,1)}), bf16[2,2048,768]{2,1,0:T(8,128)(2,1)}) %all-gather.2.cloned.1.call-update) | async-done | bytes 6291472 | tf_op jit(solution)/shard_map/all_gather | solution.py:219
  168.0 6.0 %gather_fusion = bf16[12,2,128,768]{3,2,1,0:T(8,128)(2,1)} fusion(bf16[2,16,128,768]{3,2,1,0:T(8,128)(2,1)} %bitcast.198, s32[1024]{0:T(1024)S(1)} %pad_clamp_fusion), kind=kCustom, calls=%fused_computation | custom fusion | bytes 9437232 | tf_op jit(solution)/shard_map/gather | solution.py:207
  174.0 5.0 %fusion.55 = (bf16[1,2,6,128,768]{4,3,0,2,1:T(8,128)(2,1)}, bf16[1,2,6,128,768]{4,3,0,2,1:T(8,128)(2,1)}) fusion(bf16[2,2,6,128,768]{4,3,0,2,1:T(8,128)(2,1)} %bitcast.197), kind=kLoop, calls=%fused_computation.106 | loop fusion | bytes 9437184 | tf_op jit(solution)/shard_map/slice | solution.py:239
  179.0 4.8 %copy.199 = bf16[1,2,6,128,768]{3,2,4,1,0:T(8,128)(2,1)} copy(bf16[1,2,6,128,768]{4,3,0,2,1:T(8,128)(2,1)} %get-tuple-element.21) | data formatting | bytes 4718592 | tf_op jit(solution)/shard_map/slice | solution.py:239
  183.8 6.0 %reshape.265 = bf16[2,768,12,64]{1,3,2,0:T(8,128)(2,1)} reshape(bf16[1,2,6,128,768]{3,2,4,1,0:T(8,128)(2,1)} %copy.199) | data formatting | bytes 4718592 | tf_op jit(solution)/shard_map/reshape.11
  189.8 4.8 %copy.206 = bf16[1,2,6,128,768]{3,2,4,1,0:T(8,128)(2,1)} copy(bf16[1,2,6,128,768]{4,3,0,2,1:T(8,128)(2,1)} %get-tuple-element.22) | data formatting | bytes 4718592 | tf_op jit(solution)/shard_map/slice | solution.py:240
  194.6 6.0 %reshape.266 = bf16[2,768,12,64]{1,3,2,0:T(8,128)(2,1)} reshape(bf16[1,2,6,128,768]{3,2,4,1,0:T(8,128)(2,1)} %copy.206) | data formatting | bytes 4718592 | tf_op jit(solution)/shard_map/reshape.16
  200.6 3.8 bitcast_reduce_fusion
  204.5 2.0 fusion.3
  207.2 1.5 fusion.27
  208.7 2.6 convolution_bitcast_fusion.8
  211.7 1.2 multiply_reduce_fusion
  213.5 4.1 %fusion.1 = bf16[2,12,128,768]{2,3,1,0:T(8,128)(2,1)S(1)} fusion(f32[2,12,768,128]{3,2,1,0:T(8,128)S(1)} %get-tuple-element.28, f32[2,12,128]{2,1,0:T(8,128)S(1)} %bitcast.210, f32[2,12,128]{2,1,0:T(8,128)S(1)} %log_add_fusion, pred[2,768]{1,0:T(4,128)(4,1)S(1)} %bitcast.215, bf16[2,768,12,64]{1,3,2,0:T(8,128)(2,1)S(1)} %copy-done.14, ...), kind=kOutput, calls=%fused_computation.5 | convolution fusion | flops 318504960 | bytes 16934400 | tf_op jit(solution)/shard_map/vmap(bqhd,bkhd->hbqk)/dot_general | solution.py:60
  217.7 4.1 %convolution_bitcast_fusion = f32[2,1,768,12,64]{2,4,3,0,1:T(8,128)} fusion(f32[2,12,768,128]{3,2,1,0:T(8,128)S(1)} %get-tuple-element.28, f32[2,12,128]{2,1,0:T(8,128)S(1)} %log_add_fusion, pred[2,768]{1,0:T(4,128)(4,1)S(1)} %bitcast.216, bf16[2,128,12,64]{1,0,3,2:T(2,128)(2,1)S(1)} %reshape_reshape.5), kind=kOutput, calls=%fused_computation.16 | convolution fusion | flops 311427072 | bytes 14562816 | tf_op jit(solution)/shard_map/vmap(hbqk,bqhd->bkhd)/dot_general | solution.py:138
  222.5 4.0 convolution_bitcast_fusion.1
  226.5 6.6 %reshape.270 = f32[2,6,128,768]{2,1,3,0:T(8,128)} reshape(f32[2,1,768,12,64]{2,4,3,0,1:T(8,128)} %convolution_bitcast_fusion.1) | data formatting | bytes 9437184 | tf_op jit(solution)/shard_map/vmap()/reshape | solution.py:140
  233.0 6.6 %pad_maximum_fusion.1 = f32[2,7,128,768]{2,1,3,0:T(8,128)} fusion(f32[2,1,128,768]{2,1,3,0:T(1,128)S(1)} %bitcast.200, f32[2,6,128,768]{2,1,3,0:T(8,128)} %reshape.270), kind=kLoop, calls=%fused_computation.14 | loop fusion | flops 1376256 | bytes 11010048 | tf_op jit(solution)/shard_map/vmap()/concatenate | solution.py:198
  239.7 6.3 %copy.234 = f32[2,7,128,768]{3,2,1,0:T(8,128)} copy(f32[2,7,128,768]{2,1,3,0:T(8,128)} %pad_maximum_fusion.1) | data formatting | bytes 11010048 | tf_op jit(solution)/shard_map/vmap()/concatenate | solution.py:198
  246.0 6.7 %reshape.272 = f32[2,6,128,768]{2,1,3,0:T(8,128)} reshape(f32[2,1,768,12,64]{2,4,3,0,1:T(8,128)} %convolution_bitcast_fusion) | data formatting | bytes 9437184 | tf_op jit(solution)/shard_map/vmap()/reshape | solution.py:140
  252.7 6.6 %pad_maximum_fusion.2 = f32[2,7,128,768]{2,1,3,0:T(8,128)} fusion(f32[2,1,128,768]{2,1,3,0:T(1,128)S(1)} %bitcast.199, f32[2,6,128,768]{2,1,3,0:T(8,128)} %reshape.272), kind=kLoop, calls=%fused_computation.15 | loop fusion | flops 1376256 | bytes 11010048 | tf_op jit(solution)/shard_map/vmap()/concatenate | solution.py:199
  259.3 6.4 %copy.240 = f32[2,7,128,768]{3,2,1,0:T(8,128)} copy(f32[2,7,128,768]{2,1,3,0:T(8,128)} %pad_maximum_fusion.2) | data formatting | bytes 11010048 | tf_op jit(solution)/shard_map/vmap()/concatenate | solution.py:199
  265.7 5.4 %pad_maximum_fusion = f32[14,2,128,768]{3,2,0,1:T(8,128)S(1)} fusion(f32[14,1,128,768]{3,2,0,1:T(8,128)} %bitcast.196, f32[14,1,128,768]{3,2,0,1:T(8,128)} %bitcast.195), kind=kLoop, calls=%fused_computation.2 | loop fusion | flops 2752512 | bytes 22020096 | tf_op jit(solution)/shard_map/vmap()/stack | solution.py:196
  271.1 5.3 %copy.241 = f32[14,2,128,768]{3,2,1,0:T(8,128)} copy(f32[14,2,128,768]{3,2,0,1:T(8,128)S(1)} %pad_maximum_fusion) | data formatting | bytes 22020096 | tf_op jit(solution)/shard_map/vmap()/stack | solution.py:196
  276.4 6.0 %broadcast_in_dim.84 = f32[16,2,128,768]{3,2,1,0:T(8,128)} broadcast(f32[]{:T(128)} %constant.58.clone.1), dimensions={} | broadcast | bytes 12582916 | tf_op jit(solution)/shard_map/broadcast_in_dim | solution.py:266
  282.4 25.1 %scatter_fusion = f32[16,2,128,768]{3,2,1,0:T(8,128)} fusion(f32[16,2,128,768]{3,2,1,0:T(8,128)} %broadcast_in_dim.84, s32[14]{0:T(128)S(1)} %copy-done.26, f32[14,2,128,768]{3,2,1,0:T(8,128)} %copy.241), kind=kCustom, calls=%fused_computation.1 | custom fusion | flops 2752512 | bytes 33030200 | tf_op jit(solution)/shard_map/scatter-add | solution.py:268
  307.5 8.0 %convert_element_type.66 = bf16[16,2,128,768]{3,2,1,0:T(8,128)(2,1)} convert(f32[16,2,128,768]{3,2,1,0:T(8,128)} %scatter_fusion) | non-fusion elementwise | flops 3145728 | bytes 18874368 | tf_op jit(solution)/shard_map/convert_element_type | solution.py:268
  316.9 1.5 stack.29
  318.4 2.3 copy.228
  320.7 1.3 multiply_convert_fusion
  322.0 0.9 copy-done.9
  323.5 1.5 copy.223
  325.0 2.7 stack.28
  327.7 2.4 copy.227
  330.5 0.9 copy.242
  331.5 1.4 convolution_bitcast_fusion.2
  332.9 3.8 convolution_bitcast_fusion.6
  337.5 0.9 copy.243
  338.5 60.0 %reduce-scatter.2.cloned.1.call-done = bf16[1,2,128,768]{3,2,1,0:T(8,128)(2,1)} async-done(((bf16[16,2,128,768]{3,2,1,0:T(8,128)(2,1)}), bf16[1,2,128,768]{3,2,1,0:T(8,128)(2,1)}) %reduce-scatter.2.cloned.1.call-update) | async-done | bytes 393232 | tf_op jit(solution)/shard_map/reduce_scatter | solution.py:267
  398.5 1.1 fusion.22
  399.6 0.9 copy-done.20
  (97 shorter events, 12.8 us)
Async XLA Ops:
  7.2 9.7 %copy-start.17 = (bf16[2,256,768]{2,1,0:T(8,128)(2,1)S(1)}, bf16[2,256,768]{2,1,0:T(8,128)(2,1)}, u32[]{:S(2)}) copy-start(bf16[2,256,768]{2,1,0:T(8,128)(2,1)} %param.6) | copy-start | bytes 2359300
  7.2 94.2 %all-reduce.3.cloned.1.call-start = ((), (), s32[]{:S(2)}) async-start(), calls=%async_computation.1 | async-start | bytes 786432 | tf_op jit(solution)/shard_map/psum | solution.py:15
  9.9 158.0 %all-gather.2.cloned.1.call-start = ((), (), s32[]{:S(2)}) async-start(), calls=%async_computation.2 | async-start | bytes 6684672 | tf_op jit(solution)/shard_map/all_gather | solution.py:219
  10.7 387.9 %reduce-scatter.2.cloned.1.call-start = ((), (), s32[]{:S(2)}) async-start(), calls=%async_computation.3 | async-start | bytes 6684672 | tf_op jit(solution)/shard_map/reduce_scatter | solution.py:267
  14.2 190.3 %copy-start.22 = (pred[1,2,6,128]{3,1,2,0:T(4,128)(4,1)}, pred[1,2,6,128]{3,1,2,0:T(4,128)(4,1)S(1)}, u32[]{:S(2)}) copy-start(pred[1,2,6,128]{3,1,2,0:T(4,128)(4,1)S(1)} %copy.309) | copy-start | bytes 4612
  15.5 87.0 %copy-start.2 = (bf16[2,128,12,64]{1,0,3,2:T(2,128)(2,1)}, bf16[2,128,12,64]{1,0,3,2:T(2,128)(2,1)S(1)}, u32[]{:S(2)}) copy-start(bf16[2,128,12,64]{1,0,3,2:T(2,128)(2,1)S(1)} %reshape_reshape.4) | copy-start | bytes 1179652
  18.3 85.8 %copy-start.18 = (bf16[2,128,12,64]{1,0,3,2:T(2,128)(2,1)}, bf16[2,128,12,64]{1,0,3,2:T(2,128)(2,1)S(1)}, u32[]{:S(2)}) copy-start(bf16[2,128,12,64]{1,0,3,2:T(2,128)(2,1)S(1)} %reshape_reshape_squeeze.4) | copy-start | bytes 1179652
  200.6 3.8 copy-start.24
  200.6 3.8 copy-start.25
  206.5 2.2 copy-start.14
  206.5 2.2 copy-start.23
  208.7 2.6 copy-start.11
  208.7 3.0 copy-start.15
  212.9 0.6 copy-start.21
  213.5 8.3 %copy-start.5 = (bf16[2,12,128,128]{2,3,1,0:T(8,128)(2,1)}, bf16[2,12,128,128]{2,3,1,0:T(8,128)(2,1)S(1)}, u32[]{:S(2)}) copy-start(bf16[2,12,128,128]{2,3,1,0:T(8,128)(2,1)S(1)} %fusion.8) | copy-start | bytes 2359300
  217.7 4.8 %copy-start.1 = (bf16[2,12,128,768]{2,3,1,0:T(8,128)(2,1)}, bf16[2,12,128,768]{2,3,1,0:T(8,128)(2,1)S(1)}, u32[]{:S(2)}) copy-start(bf16[2,12,128,768]{2,3,1,0:T(8,128)(2,1)S(1)} %fusion.1) | copy-start | bytes 14155780
  217.7 4.1 %copy-start.3 = (bf16[2,128,12,64]{1,0,3,2:T(2,128)(2,1)S(1)}, bf16[2,128,12,64]{1,0,3,2:T(2,128)(2,1)}, u32[]{:S(2)}) copy-start(bf16[2,128,12,64]{1,0,3,2:T(2,128)(2,1)} %copy-done.2) | copy-start | bytes 1179652
  246.0 6.7 %copy-start.13 = (f32[2,12,128,64]{2,3,1,0:T(8,128)S(1)}, f32[2,12,128,64]{2,3,1,0:T(8,128)}, u32[]{:S(2)}) copy-start(f32[2,12,128,64]{2,3,1,0:T(8,128)} %fusion.27) | copy-start | bytes 2359300
  276.4 6.0 %copy-start.26 = (s32[14]{0:T(128)S(1)}, s32[14]{0:T(128)}, u32[]{:S(2)}) copy-start(s32[14]{0:T(128)} %fusion.50) | copy-start | bytes 172
  315.6 5.1 %copy-start.12 = (bf16[2,128,12,64]{1,0,3,2:T(2,128)(2,1)S(1)}, bf16[2,128,12,64]{1,0,3,2:T(2,128)(2,1)}, u32[]{:S(2)}) copy-start(bf16[2,128,12,64]{1,0,3,2:T(2,128)(2,1)} %reshape_reshape_squeeze.10) | copy-start | bytes 1179652
  315.6 7.3 %copy-start.4 = (bf16[2,128,12,64]{1,0,3,2:T(2,128)(2,1)S(1)}, bf16[2,128,12,64]{1,0,3,2:T(2,128)(2,1)}, u32[]{:S(2)}) copy-start(bf16[2,128,12,64]{1,0,3,2:T(2,128)(2,1)} %copy-done.2) | copy-start | bytes 1179652
  322.0 0.9 copy-start.9
  322.9 7.2 %copy-start.19 = (bf16[2,128,12,64]{1,3,2,0:T(8,128)(2,1)S(1)}, bf16[2,128,12,64]{1,3,2,0:T(8,128)(2,1)}, u32[]{:S(2)}) copy-start(bf16[2,128,12,64]{1,3,2,0:T(8,128)(2,1)} %get-tuple-element.34) | copy-start | bytes 1179652
  323.5 8.0 %copy-start.10 = (bf16[2,12,128,128]{2,3,1,0:T(8,128)(2,1)S(1)}, bf16[2,12,128,128]{2,3,1,0:T(8,128)(2,1)}, u32[]{:S(2)}) copy-start(bf16[2,12,128,128]{2,3,1,0:T(8,128)(2,1)} %copy-done.9) | copy-start | bytes 2359300
  323.5 9.4 %copy-start = (bf16[2,768,12,64]{1,3,2,0:T(8,128)(2,1)S(1)}, bf16[2,768,12,64]{1,3,2,0:T(8,128)(2,1)}, u32[]{:S(2)}) copy-start(bf16[2,768,12,64]{1,3,2,0:T(8,128)(2,1)} %reshape.265) | copy-start | bytes 7077892
  331.5 5.2 %copy-start.6 = (bf16[2,12,128,128]{2,3,1,0:T(8,128)(2,1)S(1)}, bf16[2,12,128,128]{2,3,1,0:T(8,128)(2,1)}, u32[]{:S(2)}) copy-start(bf16[2,12,128,128]{2,3,1,0:T(8,128)(2,1)} %copy-done.5) | copy-start | bytes 2359300
  331.5 5.3 %copy-start.16 = (bf16[1,128,768]{1,2,0:T(8,128)(2,1)S(1)}, bf16[1,128,768]{1,2,0:T(8,128)(2,1)}, u32[]{:S(2)}) copy-start(bf16[1,128,768]{1,2,0:T(8,128)(2,1)} %copy.196) | copy-start | bytes 589828
  332.9 5.5 %copy-start.7 = (f32[1,256,768]{2,1,0:T(8,128)S(1)}, f32[1,256,768]{2,1,0:T(8,128)}, u32[]{:S(2)}) copy-start(f32[1,256,768]{2,1,0:T(8,128)} %copy.228) | copy-start | bytes 2359300
  336.7 1.7 copy-start.8
  399.6 0.9 copy-start.20
Sparse Core Ops, SparseCore 0:
  11.9 89.4 all-reduce.2
  104.5 63.3 all-gather.1
  315.7 82.8 reduce-scatter.1
where the time goes:
time: 411 us; the launch traced here: 407 us
  waiting for transfers between devices  204 us (50%)
  local copies, waits for them, and re-layouts  93.2 us (23%)
  other arithmetic  60.9 us (15%)
  matrix products  34.2 us (8%)
  between operations  14.9 us (4%)
    psum x1, waiting for transfers between devices, spread(): return lax.psum(jnp.where(mine, shard, jnp.zeros_like(shard)), axis)  81.2 us
    all_gather x1, waiting for transfers between devices, shards(): lax.all_gather(own_anchor, 'seq', axis=1, tiled=True)  61.7 us
    reduce_scatter x1, waiting for transfers between devices, shards(): lax.psum_scatter(empty.at[targets].add(flat_entries, mode='drop').astype(...  60 us
    scatter-add x1, other arithmetic, shards(): empty.at[targets].add(flat_entries, mode='drop').astype(jnp.bfloat16)  25.1 us
    reshape x2, local copies, waits for them, and re-layouts, key_side(): anchor_part = jnp.einsum('hbqk,bqhd->bkhd', anchor_weights, left_blocks,...  13.3 us
    another operation x2, local copies, waits for them, and re-layouts  12 us
    slice x2, local copies, waits for them, and re-layouts, shards(): picked[0]  9.83 us
    another operation x4, local copies, waits for them, and re-layouts, backward_span(): local_grads = jnp.stack((key_grads[0], value_grads[0]))  8.86 us
  transfers between devices with their start and end apart: 3, of which 3 were waited for; matrix products, arithmetic and copies ran while one was open for 9% of the time, Pallas kernels for 0%

commit v1 on v0

v1 whole, which is shorter than its diff:
```python
import functools
import math

import jax
import jax.numpy as jnp
from jax import lax
from jax.experimental import pallas as pl
from jax.experimental.pallas import tpu as pltpu
from jax.sharding import PartitionSpec as P

HEAD = 64
BLK = 128
PAIR = 2 * HEAD
NEG = -1e30
VMEM_BYTES = 60 * 1024 * 1024


def anchor_span(device_id, axis_length):
    return jnp.where(device_id % 2 == 0, device_id, 2 * axis_length - 1 - device_id)


def stack_heads(rows, low):
    zero = jnp.zeros_like(rows)
    return jnp.concatenate((jnp.where(low, rows, zero), jnp.where(low, zero, rows)), axis=0)


def unstack_heads(rows, low):
    return jnp.where(low, rows[:BLK], rows[BLK:])


def dot_last(left, right):
    return lax.dot_general(left, right, (((1,), (1,)), ((), ())), preferred_element_type=jnp.float32)


def dot_first(left, right):
    return lax.dot_general(left, right, (((0,), (0,)), ((), ())), preferred_element_type=jnp.float32)


def attention_kernel(
    axis_length,
    frames_ref,
    sink_ref,
    q_ref,
    kv_ref,
    g_ref,
    anchors_ref,
    out_ref,
    grad_q_ref,
    local_ref,
    parts_ref,
):
    me = lax.axis_index("seq")
    sink = sink_ref[0]
    entries = frames_ref.shape[1]
    pairs = q_ref.shape[1] // PAIR
    scale = 1.0 / math.sqrt(HEAD)
    low = lax.broadcasted_iota(jnp.int32, (BLK, PAIR), 1) < HEAD
    row = lax.broadcasted_iota(jnp.int32, (2 * BLK, BLK), 0) % BLK
    causal = lax.broadcasted_iota(jnp.int32, (2 * BLK, BLK), 1) <= row

    @pl.loop(0, axis_length)
    def _(j):
        parts_ref[j] = jnp.zeros(parts_ref.shape[1:], parts_ref.dtype)

    for block in range(2):
        span = me if block == 0 else 2 * axis_length - 1 - me
        rows = pl.ds(block * BLK, BLK)
        ids = [frames_ref[block, e] for e in range(entries)]
        biases = []
        for e in range(entries):
            valid = (anchor_span(ids[e], axis_length) < span) & (ids[e] != sink)
            for earlier in range(e):
                valid = valid & (ids[e] != ids[earlier])
            biases.append(jnp.where(valid, 0.0, NEG))
        biases.append(None)
        slots = ids + [sink]
        window_scalar = jnp.where(span == anchor_span(sink, axis_length), NEG, 0.0)
        window_bias = jnp.where(causal, window_scalar, NEG)

        @pl.loop(0, pairs)
        def _(pair):
            cols = pl.ds(pl.multiple_of(pair * PAIR, PAIR), PAIR)
            q2 = stack_heads(q_ref[rows, cols] * jnp.bfloat16(scale), low)
            grad = g_ref[rows, cols]
            g2 = stack_heads(grad, low)
            keys = jnp.concatenate(
                [kv_ref[0, rows, cols]] + [anchors_ref[j, 0, :, cols] for j in slots], axis=0
            )
            values = jnp.concatenate(
                [kv_ref[1, rows, cols]] + [anchors_ref[j, 1, :, cols] for j in slots], axis=0
            )
            tiles = 1 + len(slots)
            scores = dot_last(q2, keys)
            parts = [scores[:, t * BLK : (t + 1) * BLK] for t in range(tiles)]
            parts[0] = parts[0] + window_bias
            for t in range(1, tiles - 1):
                parts[t] = parts[t] + biases[t - 1]
            top = functools.reduce(jnp.maximum, parts)
            top = jnp.max(top, axis=1, keepdims=True)
            weights = [jnp.exp(part - top) for part in parts]
            total = jnp.sum(functools.reduce(jnp.add, weights), axis=1, keepdims=True)
            inverse = 1.0 / total
            weights = [w * inverse for w in weights]
            weights_low = jnp.concatenate([w.astype(jnp.bfloat16) for w in weights], axis=1)
            out2 = jnp.dot(weights_low, values, preferred_element_type=jnp.float32)
            attended = unstack_heads(out2, low).astype(jnp.bfloat16)
            out_ref[rows, cols] = attended
            product = grad.astype(jnp.float32) * attended.astype(jnp.float32)
            delta = jnp.sum(stack_heads(product, low), axis=1, keepdims=True)
            dprobs = dot_last(g2, values)
            dscores = jnp.concatenate(
                [
                    (weights[t] * (dprobs[:, t * BLK : (t + 1) * BLK] - delta)).astype(jnp.bfloat16)
                    for t in range(tiles)
                ],
                axis=1,
            )
            grad2 = jnp.dot(dscores, keys, preferred_element_type=jnp.float32)
            grad_q_ref[rows, cols] = (unstack_heads(grad2, low) * scale).astype(jnp.bfloat16)
            for which, product in ((0, dot_first(dscores, q2)), (1, dot_first(weights_low, g2))):
                local_ref[which, rows, cols] = product[:BLK]
                for t in range(1, tiles):
                    j = slots[t - 1]
                    held = parts_ref[j, which, :, cols].astype(jnp.float32)
                    parts_ref[j, which, :, cols] = (
                        held + product[t * BLK : (t + 1) * BLK]
                    ).astype(jnp.bfloat16)


def attention(axis_length, frames, sink, queries, keys_values, cotangent, anchors):
    vmem = pl.BlockSpec(memory_space=pltpu.VMEM)
    smem = pl.BlockSpec(memory_space=pltpu.SMEM)
    return pl.pallas_call(
        functools.partial(attention_kernel, axis_length),
        out_shape=(
            jax.ShapeDtypeStruct(queries.shape, jnp.bfloat16),
            jax.ShapeDtypeStruct(queries.shape, jnp.bfloat16),
            jax.ShapeDtypeStruct(keys_values.shape, jnp.float32),
            jax.ShapeDtypeStruct(anchors.shape, jnp.bfloat16),
        ),
        in_specs=[smem, smem, vmem, vmem, vmem, vmem],
        out_specs=[vmem] * 4,
        compiler_params=pltpu.CompilerParams(vmem_limit_bytes=VMEM_BYTES),
        name="attention",
    )(frames, sink, queries, keys_values, cotangent, anchors)


def shards(queries, keys_values, cotangent, frame_lists, sink_owner):
    axis_length = lax.axis_size("seq")
    me = lax.axis_index("seq")
    offset = jnp.where(me % 2 == 0, 0, BLK).astype(jnp.int32)
    own_anchor = lax.dynamic_slice_in_dim(keys_values, offset, BLK, axis=1)
    anchors = lax.all_gather(own_anchor, "seq", axis=0, tiled=False)
    attended, grad_queries, local, parts = attention(
        axis_length, frame_lists, sink_owner, queries, keys_values, cotangent, anchors
    )
    reduced = lax.psum_scatter(parts, "seq", scatter_dimension=0, tiled=True)[0]
    anchor_rows = lax.dynamic_slice_in_dim(local, offset, BLK, axis=1) + reduced.astype(jnp.float32)
    local = lax.dynamic_update_slice_in_dim(local, anchor_rows, offset, axis=1)
    return attended, grad_queries, local.astype(jnp.bfloat16)


def solution(mesh):
    rows = P(("groups", "seq"), None)
    pairs = P(None, ("groups", "seq"), None)
    return jax.shard_map(
        shards,
        mesh=mesh,
        in_specs=(rows, pairs, rows, rows, P("groups")),
        out_specs=(rows, rows, pairs),
        check_vma=False,
    )
```

time: 411 us -> 194 us (0.47)
  local copies, waits for them, and re-layouts: 93.2 us -> 1.78 us
  other arithmetic: 60.9 us -> 2.07 us
  waiting for transfers between devices: 204 us -> 147 us
  matrix products: 34.2 us -> 0 us
  Pallas kernels: 0 us -> 25 us
    psum x1 -> x0, waiting for transfers between devices: 81.2 us -> none  [spread(): return lax.psum(jnp.where(mine, shard, jnp.zeros_like(shard)), axis)]
    dot_general x18 -> x0, matrix products: 34.2 us -> none  [the longest x2 8.13 us: key_side(): jnp.einsum('hbqk,bqhd->bkhd', anchor_weights, left_blocks, preferred_elem...]
    another operation x11 -> x0, local copies, waits for them, and re-layouts: 27.3 us -> none
    scatter-add x1 -> x0, other arithmetic: 25.1 us -> none  [shards(): empty.at[targets].add(flat_entries, mode='drop').astype(jnp.bfloat16)]
    pallas_call x0 -> x1, Pallas kernels: none -> 25 us  [attention(): pl.pallas_call(functools.partial(attention_kernel, axis_length), out_shap...]
    reduce_scatter x1, waiting for transfers between devices: 60 us -> 82.7 us  [shards(): reduced = lax.psum_scatter(parts, 'seq', scatter_dimension=0, tiled=True)[0]]
    slice x9 -> x0, local copies, waits for them, and re-layouts: 17.7 us -> none  [the longest x2 9.83 us: shards(): picked[0]]
    concatenate x3 -> x0, local copies, waits for them, and re-layouts: 13.4 us -> none  [the longest x1 6.36 us: backward_span(): jnp.concatenate((value_grads[2], value_grads[1][None]), axis=0)]
  transfers between devices with their start and end apart: 3 -> 2, of which waited for: 3 -> 2; matrix products, arithmetic and copies ran while one was open for 9% -> 0% of each run, Pallas kernels for 0% -> 0%
where the time goes in v1:
time: 194 us; the launch traced here: 191 us
  waiting for transfers between devices  147 us (76%)
  Pallas kernels  25 us (13%)
  between operations  14.7 us (8%)
  other arithmetic  2.07 us (1%)
    reduce_scatter x1, waiting for transfers between devices, shards(): reduced = lax.psum_scatter(parts, 'seq', scatter_dimension=0, tiled=True)[0]  82.7 us
    all_gather x1, waiting for transfers between devices, shards(): anchors = lax.all_gather(own_anchor, 'seq', axis=0, tiled=False)  64.6 us
    pallas_call x1, Pallas kernels, attention(): pl.pallas_call(functools.partial(attention_kernel, axis_length), out_shap...  25 us
  transfers between devices with their start and end apart: 2, of which 2 were waited for; matrix products, arithmetic and copies ran while one was open for 0% of the time, Pallas kernels for 0%

profile of v1, /device:TPU:11, one launch (start us, length us, event | category | flops | bytes accessed | tf_op | source)
XLA Modules:
  0.0 190.9 jit_solution(10802071187316262586)
XLA Ops:
  7.2 0.0 all-gather.3.cloned.1.call-start
  7.2 1.8 constant_dynamic-slice_fusion
  9.0 0.0 all-gather.3.cloned.1.call-update
  9.0 0.0 reduce-scatter.2.cloned.1.call-start
  9.7 64.6 %all-gather.3.cloned.1.call-done = bf16[32,128,768]{2,1,0:T(8,128)(2,1)} async-done(((bf16[2,128,768]{2,1,0:T(8,128)(2,1)}), bf16[32,128,768]{2,1,0:T(8,128)(2,1)}) %all-gather.3.cloned.1.call-update) | async-done | bytes 6291472 | tf_op jit(solution)/shard_map/all_gather | solution.py:153
  74.3 25.0 %attention.1 = (bf16[256,768]{1,0:T(8,128)(2,1)}, bf16[256,768]{1,0:T(8,128)(2,1)}, f32[2,256,768]{2,1,0:T(8,128)}, bf16[16,2,128,768]{3,2,1,0:T(8,128)(2,1)}) custom-call(s32[2,6]{1,0:T(2,128)} %frames_ref.1, s32[1]{0:T(128)S(6)} %copy.9.sink_ref, bf16[256,768]{1,0:T(8,128)(2,1)} %q_ref.1, bf16[2,256,768]{2,1,0:T(8,128)(2,1)} %kv_ref.1, ...), custom_call_target="tpu_custom_call" | custom-call | tf_op jit(solution)/shard_map/attention/pallas_call | solution.py:133
  99.3 0.0 copy-start
  99.3 0.0 reduce-scatter.2.cloned.1.call-update
  99.3 82.7 %reduce-scatter.2.cloned.1.call-done = bf16[1,2,128,768]{3,2,1,0:T(8,128)(2,1)} async-done(((bf16[16,2,128,768]{3,2,1,0:T(8,128)(2,1)}), bf16[1,2,128,768]{3,2,1,0:T(8,128)(2,1)}) %reduce-scatter.2.cloned.1.call-update) | async-done | bytes 393232 | tf_op jit(solution)/shard_map/reduce_scatter | solution.py:157
  181.9 0.0 copy-done
  181.9 1.1 fusion
  183.1 1.0 convert_element_type.11
Async XLA Ops:
  7.2 67.1 %all-gather.3.cloned.1.call-start = ((), (), s32[]{:S(2)}) async-start(), calls=%async_computation.2 | async-start | bytes 6684672 | tf_op jit(solution)/shard_map/all_gather | solution.py:153
  9.0 172.9 %reduce-scatter.2.cloned.1.call-start = ((), (), s32[]{:S(2)}) async-start(), calls=%async_computation.1 | async-start | bytes 6684672 | tf_op jit(solution)/shard_map/reduce_scatter | solution.py:157
  99.3 82.7 %copy-start = (f32[2,256,768]{2,1,0:T(8,128)S(1)}, f32[2,256,768]{2,1,0:T(8,128)}, u32[]{:S(2)}) copy-start(f32[2,256,768]{2,1,0:T(8,128)} %get-tuple-element.9) | copy-start | bytes 4718596
Sparse Core Ops, SparseCore 0:
  10.9 63.3 all-gather.2
  99.4 82.4 reduce-scatter.1

commit v2 on v1

--- a/solution.py
+++ b/solution.py
@@ -145,26 +145,334 @@
     )(frames, sink, queries, keys_values, cotangent, anchors)
 
 
-def shards(queries, keys_values, cotangent, frame_lists, sink_owner):
+def gather_kernel(
+    axis_length, y_count, kv_ref, out_ref, own_sem, up_sem, down_sem, y_sem, core_sem, recv_sem
+):
+    z_count = axis_length // (2 * y_count)
+    me = lax.axis_index("seq")
+    core = me % 2
+    y = (me // 2) % y_count
+    z = me // (2 * y_count)
+    y_peer = (z * y_count + (y_count - 1 - y)) * 2 + core
+    sibling = me + 1 - 2 * core
+    offset = core * BLK
+
+    def index(z_at, y_at, core_at):
+        return (z_at * y_count + y_at) * 2 + core_at
+
+    barrier = pltpu.get_barrier_semaphore()
+
+    for k in range(1, z_count):
+        pl.semaphore_signal(
+            barrier, inc=1, device_id={"seq": index((z + k) % z_count, y, core)}
+        )
+    peers = z_count
+    pl.semaphore_signal(barrier, inc=1, device_id={"seq": sibling})
+    if y_count > 1:
+        pl.semaphore_signal(barrier, inc=1, device_id={"seq": y_peer})
+        peers += 1
+    pl.semaphore_wait(barrier, peers)
+
+    def remote(piece, which, target, send_sem, own=False):
+        place = out_ref.at[piece, which]
+        source = kv_ref.at[which, pl.ds(offset, BLK)] if own else place
+        return pltpu.make_async_remote_copy(
+            src_ref=source,
+            dst_ref=place,
+            send_sem=send_sem,
+            recv_sem=recv_sem.at[piece, which],
+            device_id={"seq": target},
+            device_id_type=pl.DeviceIdType.MESH,
+        )
+
+    def await_piece(piece, which):
+        remote(piece, which, sibling, core_sem.at[0, which]).wait_recv()
+
+    def to_up(step, which, own=False):
+        return remote(
+            index(z - step, y, core), which, me + 2 * y_count, up_sem.at[step, which], own
+        )
+
+    def to_down(step, which, own=False):
+        return remote(
+            index(z + step, y, core), which, me - 2 * y_count, down_sem.at[step, which], own
+        )
+
+    def to_y(z_at, which, own=False):
+        return remote(index(z_at, y, core), which, y_peer, y_sem.at[z_at, which], own)
+
+    def to_core(z_at, y_at, which, own=False):
+        return remote(
+            index(z_at, y_at, core), which, sibling, core_sem.at[z_at * y_count + y_at, which], own
+        )
+
+    def own_copy(which):
+        return pltpu.make_async_copy(
+            kv_ref.at[which, pl.ds(offset, BLK)], out_ref.at[me, which], own_sem.at[which]
+        )
+
+    for which in range(2):
+        pl.when(z < z_count - 1)(lambda: to_up(0, which, True).start())
+        pl.when(z > 0)(lambda: to_down(0, which, True).start())
+        if y_count > 1:
+            to_y(z, which, True).start()
+        to_core(z, y, which, True).start()
+    for which in range(2):
+        own_copy(which).start()
+
+    def pass_y(distance):
+        if y_count == 1:
+            return
+        for which in range(2):
+            def hand(z_at):
+                await_piece(index(z_at, 1 - y, core), which)
+                to_core(z_at, 1 - y, which).start()
+
+            pl.when(z - distance >= 0)(lambda: hand(z - distance))
+            if distance:
+                pl.when(z + distance < z_count)(lambda: hand(z + distance))
+
+    for step in range(1, z_count):
+        for which in range(2):
+            @pl.when(z - step >= 0)
+            def _():
+                await_piece(index(z - step, y, core), which)
+                pl.when(z < z_count - 1)(lambda: to_up(step, which).start())
+                if y_count > 1:
+                    to_y(z - step, which).start()
+                to_core(z - step, y, which).start()
+
+            @pl.when(z + step < z_count)
+            def _():
+                await_piece(index(z + step, y, core), which)
+                pl.when(z > 0)(lambda: to_down(step, which).start())
+                if y_count > 1:
+                    to_y(z + step, which).start()
+                to_core(z + step, y, which).start()
+        pass_y(step - 1)
+    pass_y(z_count - 1)
+
+    for which in range(2):
+        own_copy(which).wait()
+        for z_at in range(z_count):
+            for y_at in range(y_count):
+                await_piece(index(z_at, y_at, 1 - core), which)
+        for z_at in range(z_count):
+            if y_count > 1:
+                to_y(z_at, which).wait_send()
+            for y_at in range(y_count):
+                to_core(z_at, y_at, which).wait_send()
+            pl.when((z - z_at >= 0) & (z < z_count - 1))(lambda: to_up(z_at, which).wait_send())
+            pl.when((z + z_at < z_count) & (z > 0))(lambda: to_down(z_at, which).wait_send())
+
+
+def gather_anchors(axis_length, y_count, keys_values):
+    z_count = axis_length // (2 * y_count)
+    hbm = pl.BlockSpec(memory_space=pl.ANY)
+    dma = pltpu.SemaphoreType.DMA
+    return pl.pallas_call(
+        functools.partial(gather_kernel, axis_length, y_count),
+        out_shape=jax.ShapeDtypeStruct(
+            (axis_length, 2, BLK, keys_values.shape[2]), jnp.bfloat16
+        ),
+        in_specs=[hbm],
+        out_specs=hbm,
+        scratch_shapes=[
+            dma((2,)),
+            dma((z_count, 2)),
+            dma((z_count, 2)),
+            dma((z_count, 2)),
+            dma((z_count * y_count, 2)),
+            dma((axis_length, 2)),
+        ],
+        compiler_params=pltpu.CompilerParams(collective_id=0, has_side_effects=True),
+        name="gather",
+    )(keys_values)
+
+
+def reduce_kernel(
+    axis_length,
+    y_count,
+    local_ref,
+    parts_ref,
+    out_ref,
+    from_core,
+    from_y,
+    from_z,
+    core_sum,
+    z_term,
+    core_send,
+    core_recv,
+    y_send,
+    y_recv,
+    z_send,
+    z_recv,
+):
+    z_count = axis_length // (2 * y_count)
+    me = lax.axis_index("seq")
+    core = me % 2
+    y = (me // 2) % y_count
+    z = me // (2 * y_count)
+    other_y = y_count - 1 - y
+    y_peer = (z * y_count + other_y) * 2 + core
+    sibling = me + 1 - 2 * core
+    offset = core * BLK
+    stride = jnp.where(z < z_count // 2, -1, 1)
+    order = [(z + stride * (1 + k) + z_count) % z_count for k in range(z_count)]
+
+    barrier = pltpu.get_barrier_semaphore()
+    peers = z_count - 1 + y_count
+    for k in range(z_count - 1):
+        pl.semaphore_signal(
+            barrier, inc=1, device_id={"seq": (order[k] * y_count + y) * 2 + core}
+        )
+    pl.semaphore_signal(barrier, inc=1, device_id={"seq": sibling})
+    if y_count > 1:
+        pl.semaphore_signal(barrier, inc=1, device_id={"seq": y_peer})
+    pl.semaphore_wait(barrier, peers)
+
+    def remote(source, place, send_sem, recv_sem, target):
+        return pltpu.make_async_remote_copy(
+            src_ref=source,
+            dst_ref=place,
+            send_sem=send_sem,
+            recv_sem=recv_sem,
+            device_id={"seq": target},
+            device_id_type=pl.DeviceIdType.MESH,
+        )
+
+    def to_core(piece):
+        return remote(
+            parts_ref.at[piece * 2 + 1 - core],
+            from_core.at[piece],
+            core_send.at[piece],
+            core_recv.at[piece],
+            sibling,
+        )
+
+    def to_y(k, which):
+        return remote(
+            core_sum.at[order[k] * y_count + other_y, which],
+            from_y.at[order[k], which],
+            y_send.at[k, which],
+            y_recv.at[k, which],
+            y_peer,
+        )
+
+    def to_z(k, which):
+        return remote(
+            z_term.at[order[k], which],
+            from_z.at[z, which],
+            z_send.at[k, which],
+            z_recv.at[z, which],
+            (order[k] * y_count + y) * 2 + core,
+        )
+
+    def from_z_wait(k, which):
+        remote(
+            z_term.at[order[k], which],
+            from_z.at[order[k], which],
+            z_send.at[k, which],
+            z_recv.at[order[k], which],
+            sibling,
+        ).wait_recv()
+
+    def wide(value):
+        return value.astype(jnp.float32)
+
+    def merge_core(piece):
+        to_core(piece).wait_recv()
+        for which in range(2):
+            core_sum[piece, which] = (
+                wide(parts_ref[piece * 2 + core, which]) + wide(from_core[piece, which])
+            ).astype(jnp.bfloat16)
+
+    if y_count > 1:
+        for k in range(z_count):
+            to_core(order[k] * y_count + other_y).start()
+    for k in range(z_count):
+        to_core(order[k] * y_count + y).start()
+    if y_count > 1:
+        for k in range(z_count):
+            merge_core(order[k] * y_count + other_y)
+            for which in range(2):
+                to_y(k, which).start()
+    for k in range(z_count):
+        merge_core(order[k] * y_count + y)
+    rest = (1 - core) * BLK
+    for which in range(2):
+        out_ref[which, pl.ds(rest, BLK)] = local_ref[which, pl.ds(rest, BLK)].astype(jnp.bfloat16)
+    for k in range(z_count):
+        for which in range(2):
+            term = wide(core_sum[order[k] * y_count + y, which])
+            if y_count > 1:
+                to_y(k, which).wait_recv()
+                term = term + wide(from_y[order[k], which])
+            if k < z_count - 1:
+                z_term[order[k], which] = term.astype(jnp.bfloat16)
+                to_z(k, which).start()
+            else:
+                total = term + local_ref[which, pl.ds(offset, BLK)]
+                for other in range(z_count - 1):
+                    from_z_wait(other, which)
+                    total = total + wide(from_z[order[other], which])
+                out_ref[which, pl.ds(offset, BLK)] = total.astype(jnp.bfloat16)
+    for k in range(z_count):
+        for y_at in range(y_count):
+            to_core(order[k] * y_count + y_at).wait_send()
+        for which in range(2):
+            if y_count > 1:
+                to_y(k, which).wait_send()
+            if k < z_count - 1:
+                to_z(k, which).wait_send()
+
+
+def reduce_parts(axis_length, y_count, local, parts):
+    z_count = axis_length // (2 * y_count)
+    chips = axis_length // 2
+    tile = parts.shape[1:]
+    vmem = pl.BlockSpec(memory_space=pltpu.VMEM)
+    dma = pltpu.SemaphoreType.DMA
+    return pl.pallas_call(
+        functools.partial(reduce_kernel, axis_length, y_count),
+        out_shape=jax.ShapeDtypeStruct(local.shape, jnp.bfloat16),
+        in_specs=[vmem, vmem],
+        out_specs=vmem,
+        scratch_shapes=[
+            pltpu.VMEM((chips,) + tile, jnp.bfloat16),
+            pltpu.VMEM((z_count,) + tile, jnp.bfloat16),
+            pltpu.VMEM((z_count,) + tile, jnp.bfloat16),
+            pltpu.VMEM((chips,) + tile, jnp.bfloat16),
+            pltpu.VMEM((z_count,) + tile, jnp.bfloat16),
+            dma((chips,)),
+            dma((chips,)),
+            dma((z_count, 2)),
+            dma((z_count, 2)),
+            dma((z_count, 2)),
+            dma((z_count, 2)),
+        ],
+        compiler_params=pltpu.CompilerParams(
+            collective_id=1, has_side_effects=True, vmem_limit_bytes=VMEM_BYTES
+        ),
+        name="reduce",
+    )(local, parts)
+
+
+def shards(y_count, queries, keys_values, cotangent, frame_lists, sink_owner):
     axis_length = lax.axis_size("seq")
-    me = lax.axis_index("seq")
-    offset = jnp.where(me % 2 == 0, 0, BLK).astype(jnp.int32)
-    own_anchor = lax.dynamic_slice_in_dim(keys_values, offset, BLK, axis=1)
-    anchors = lax.all_gather(own_anchor, "seq", axis=0, tiled=False)
+    anchors = gather_anchors(axis_length, y_count, keys_values)
     attended, grad_queries, local, parts = attention(
         axis_length, frame_lists, sink_owner, queries, keys_values, cotangent, anchors
     )
-    reduced = lax.psum_scatter(parts, "seq", scatter_dimension=0, tiled=True)[0]
-    anchor_rows = lax.dynamic_slice_in_dim(local, offset, BLK, axis=1) + reduced.astype(jnp.float32)
-    local = lax.dynamic_update_slice_in_dim(local, anchor_rows, offset, axis=1)
-    return attended, grad_queries, local.astype(jnp.bfloat16)
+    return attended, grad_queries, reduce_parts(axis_length, y_count, local, parts)
 
 
 def solution(mesh):
     rows = P(("groups", "seq"), None)
     pairs = P(None, ("groups", "seq"), None)
+    y_count = 2 if mesh.shape["groups"] == 2 and mesh.shape["seq"] % 4 == 0 else 1
     return jax.shard_map(
-        shards,
+        functools.partial(shards, y_count),
         mesh=mesh,
         in_specs=(rows, pairs, rows, rows, P("groups")),
         out_specs=(rows, rows, pairs),

time: 194 us -> 120 us (0.62); the launches traced: 191 us -> 120 us
  waiting for transfers between devices: 147 us -> 0 us
  Pallas kernels: 25 us -> 116 us
  between operations: 14.7 us -> 1.29 us
  other arithmetic: 2.07 us -> 0 us
    pallas_call x0 -> x2, Pallas kernels: none -> 91.2 us  [the longest x1 49.9 us: reduce_parts(): pl.pallas_call(functools.partial(reduce_kernel, axis_length, y_count), ou...]
    reduce_scatter x1 -> x0, waiting for transfers between devices: 82.7 us -> none  [shards(): reduced = lax.psum_scatter(parts, 'seq', scatter_dimension=0, tiled=True)[0]]
    all_gather x1 -> x0, waiting for transfers between devices: 64.6 us -> none  [shards(): anchors = lax.all_gather(own_anchor, 'seq', axis=0, tiled=False)]
    unnamed x2 -> x1, local copies, waits for them, and re-layouts: 0.01 us -> 2.06 us
  transfers between devices with their start and end apart: 2 -> 0, of which waited for: 2 -> 0; matrix products, arithmetic and copies ran while one was open for 0% -> 0% of each run, Pallas kernels for 0% -> 0%
where the time goes in v2:
time: 120 us
  Pallas kernels  116 us (97%)
  local copies, waits for them, and re-layouts  2.06 us (2%)
  between operations  1.29 us (1%)
    pallas_call x1, Pallas kernels, reduce_parts(): pl.pallas_call(functools.partial(reduce_kernel, axis_length, y_count), ou...  49.9 us
    pallas_call x1, Pallas kernels, gather_anchors(): pl.pallas_call(functools.partial(gather_kernel, axis_length, y_count), ou...  41.3 us
    pallas_call x1, Pallas kernels, attention(): pl.pallas_call(functools.partial(attention_kernel, axis_length), out_shap...  25 us

profile of v2, /device:TPU:11, one launch (start us, length us, event | category | flops | bytes accessed | tf_op | source)
XLA Modules:
  0.0 119.6 jit_solution(3983878220435491092)
XLA Ops:
  1.3 41.3 %gather.1.anchors_ref = bf16[16,2,128,768]{3,2,1,0:T(8,128)(2,1)} custom-call(bf16[2,256,768]{2,1,0:T(8,128)(2,1)} %kv_ref.3), custom_call_target="tpu_custom_call" | custom-call | tf_op jit(solution)/shard_map/gather/pallas_call | solution.py:273
  42.6 25.0 %attention.1 = (bf16[256,768]{1,0:T(8,128)(2,1)}, bf16[256,768]{1,0:T(8,128)(2,1)}, f32[2,256,768]{2,1,0:T(8,128)}, bf16[16,2,128,768]{3,2,1,0:T(8,128)(2,1)}) custom-call(s32[2,6]{1,0:T(2,128)} %frames_ref.1, s32[1]{0:T(128)S(6)} %copy.9.sink_ref, bf16[256,768]{1,0:T(8,128)(2,1)} %q_ref.1, bf16[2,256,768]{2,1,0:T(8,128)(2,1)} %kv_ref.3, ...), custom_call_target="tpu_custom_call" | custom-call | tf_op jit(solution)/shard_map/attention/pallas_call | solution.py:133
  67.6 49.9 %reduce.1 = bf16[2,256,768]{2,1,0:T(8,128)(2,1)} custom-call(f32[2,256,768]{2,1,0:T(8,128)} %get-tuple-element.9.local_ref, bf16[16,2,128,768]{3,2,1,0:T(8,128)(2,1)} %get-tuple-element.10.parts_ref), custom_call_target="tpu_custom_call" | custom-call | tf_op jit(solution)/shard_map/reduce/pallas_call | solution.py:436
  117.6 2.1 %copy.10 = bf16[2,256,768]{2,1,0:T(8,128)(2,1)} copy(bf16[2,256,768]{2,1,0:T(8,128)(2,1)} %reduce.1) | data formatting | bytes 1572864

commit v3 on v1

v3 whole, which is shorter than its diff:
```python
import functools
import math

import jax
import jax.numpy as jnp
from jax import lax
from jax.experimental import pallas as pl
from jax.experimental.pallas import tpu as pltpu
from jax.sharding import PartitionSpec as P

HEAD = 64
BLK = 128
PAIR = 2 * HEAD
NEG = -1e30
VMEM_BYTES = 60 * 1024 * 1024


def anchor_span(device_id, axis_length):
    return jnp.where(device_id % 2 == 0, device_id, 2 * axis_length - 1 - device_id)


def stack_heads(rows, low):
    zero = jnp.zeros_like(rows)
    return jnp.concatenate((jnp.where(low, rows, zero), jnp.where(low, zero, rows)), axis=0)


def unstack_heads(rows, low):
    return jnp.where(low, rows[:BLK], rows[BLK:])


def dot_last(left, right):
    return lax.dot_general(left, right, (((1,), (1,)), ((), ())), preferred_element_type=jnp.float32)


def dot_first(left, right):
    return lax.dot_general(left, right, (((0,), (0,)), ((), ())), preferred_element_type=jnp.float32)


def attend_step(
    axis_length, half, item, frames_ref, sink_ref, q_ref, kv_ref, g_ref, anchors_ref, outs
):
    out_ref, grad_q_ref, local_ref, entry_ref = outs
    me = lax.axis_index("seq")
    sink = sink_ref[0]
    entries = frames_ref.shape[1]
    pairs = anchors_ref.shape[3] // PAIR
    scale = 1.0 / math.sqrt(HEAD)
    low = lax.broadcasted_iota(jnp.int32, (BLK, PAIR), 1) < HEAD
    row = lax.broadcasted_iota(jnp.int32, (2 * BLK, BLK), 0) % BLK
    causal = lax.broadcasted_iota(jnp.int32, (2 * BLK, BLK), 1) <= row
    block = jnp.where(item >= pairs, 1, 0)
    pair = item - block * pairs
    span = jnp.where(block == 0, me, 2 * axis_length - 1 - me)
    rows = pl.ds(pl.multiple_of(block * BLK, BLK), BLK)
    ids = [frames_ref[block, e] for e in range(entries)]
    biases = []
    for e in range(entries):
        valid = (anchor_span(ids[e], axis_length) < span) & (ids[e] != sink)
        for earlier in range(e):
            valid = valid & (ids[e] != ids[earlier])
        biases.append(jnp.where(valid, 0.0, NEG))
    slots = ids + [sink]
    window_scalar = jnp.where(span == anchor_span(sink, axis_length), NEG, 0.0)
    window_bias = jnp.where(causal, window_scalar, NEG)
    cols = pl.ds(pl.multiple_of((half * pairs + pair) * PAIR, PAIR), PAIR)
    near = pl.ds(pl.multiple_of(pair * PAIR, PAIR), PAIR)
    out_cols = cols if out_ref.shape[1] == q_ref.shape[1] else near
    q2 = stack_heads(q_ref[rows, cols] * jnp.bfloat16(scale), low)
    grad = g_ref[rows, cols]
    g2 = stack_heads(grad, low)
    keys = jnp.concatenate(
        [kv_ref[0, rows, cols]] + [anchors_ref[j, 0, :, near] for j in slots], axis=0
    )
    values = jnp.concatenate(
        [kv_ref[1, rows, cols]] + [anchors_ref[j, 1, :, near] for j in slots], axis=0
    )
    tiles = 1 + len(slots)
    scores = dot_last(q2, keys)
    parts = [scores[:, t * BLK : (t + 1) * BLK] for t in range(tiles)]
    parts[0] = parts[0] + window_bias
    for t in range(1, tiles - 1):
        parts[t] = parts[t] + biases[t - 1]
    top = functools.reduce(jnp.maximum, parts)
    top = jnp.max(top, axis=1, keepdims=True)
    weights = [jnp.exp(part - top) for part in parts]
    total = jnp.sum(functools.reduce(jnp.add, weights), axis=1, keepdims=True)
    inverse = 1.0 / total
    weights = [w * inverse for w in weights]
    weights_low = jnp.concatenate([w.astype(jnp.bfloat16) for w in weights], axis=1)
    out2 = jnp.dot(weights_low, values, preferred_element_type=jnp.float32)
    attended = unstack_heads(out2, low).astype(jnp.bfloat16)
    out_ref[rows, out_cols] = attended
    product = grad.astype(jnp.float32) * attended.astype(jnp.float32)
    delta = jnp.sum(stack_heads(product, low), axis=1, keepdims=True)
    dprobs = dot_last(g2, values)
    dscores = jnp.concatenate(
        [
            (weights[t] * (dprobs[:, t * BLK : (t + 1) * BLK] - delta)).astype(jnp.bfloat16)
            for t in range(tiles)
        ],
        axis=1,
    )
    grad2 = jnp.dot(dscores, keys, preferred_element_type=jnp.float32)
    grad_q_ref[rows, out_cols] = (unstack_heads(grad2, low) * scale).astype(jnp.bfloat16)
    for which, product in ((0, dot_first(dscores, q2)), (1, dot_first(weights_low, g2))):
        local_ref[which, rows, near] = product[:BLK]
        for t in range(1, tiles):
            entry_ref[block, t - 1, which, :, near] = product[t * BLK : (t + 1) * BLK].astype(
                jnp.bfloat16
            )


def clear_entries(entry_ref, entries):
    for block in range(2):
        entry_ref[block, entries + 1] = jnp.zeros(entry_ref.shape[2:], jnp.bfloat16)


def assemble(axis_length, frames_ref, sink_ref, entry_ref, parts_ref):
    entries = frames_ref.shape[1]

    @pl.loop(0, axis_length)
    def _(j):
        picked = []
        for block in range(2):
            slot = entries + 1
            for e in reversed(range(entries)):
                slot = jnp.where(frames_ref[block, e] == j, e, slot)
            picked.append(jnp.where(sink_ref[0] == j, entries, slot))
        for which in range(2):
            parts_ref[j, which] = (
                entry_ref[0, picked[0], which].astype(jnp.float32)
                + entry_ref[1, picked[1], which].astype(jnp.float32)
            ).astype(jnp.bfloat16)


def gather_attend_kernel(
    axis_length,
    y_count,
    frames_ref,
    sink_ref,
    q_ref,
    kv_ref,
    g_ref,
    out_ref,
    grad_q_ref,
    local_ref,
    parts_ref,
    second_ref,
    first_ref,
    entry_ref,
    own_sem,
    up_sem,
    down_sem,
    y_sem,
    core_sem,
    recv_sem,
):
    z_count = axis_length // (2 * y_count)
    me = lax.axis_index("seq")
    core = me % 2
    y = (me // 2) % y_count
    z = me // (2 * y_count)
    y_peer = (z * y_count + (y_count - 1 - y)) * 2 + core
    sibling = me + 1 - 2 * core
    offset = core * BLK
    width = first_ref.shape[3]
    items = 2 * width // PAIR
    step_items = -(-items // (z_count - 1))

    def index(z_at, y_at, core_at):
        return (z_at * y_count + y_at) * 2 + core_at

    barrier = pltpu.get_barrier_semaphore()

    for k in range(1, z_count):
        pl.semaphore_signal(
            barrier, inc=1, device_id={"seq": index((z + k) % z_count, y, core)}
        )
    peers = z_count
    pl.semaphore_signal(barrier, inc=1, device_id={"seq": sibling})
    if y_count > 1:
        pl.semaphore_signal(barrier, inc=1, device_id={"seq": y_peer})
        peers += 1
    pl.semaphore_wait(barrier, peers)

    def plan(half, buffer):
        def remote(piece, which, target, send_sem, own=False):
            place = buffer.at[piece, which]
            source = kv_ref.at[which, pl.ds(offset, BLK), pl.ds(half * width, width)] if own else place
            return pltpu.make_async_remote_copy(
                src_ref=source,
                dst_ref=place,
                send_sem=send_sem,
                recv_sem=recv_sem.at[half, piece, which],
                device_id={"seq": target},
                device_id_type=pl.DeviceIdType.MESH,
            )

        def await_piece(piece, which):
            remote(piece, which, sibling, core_sem.at[half, 0, which]).wait_recv()

        def to_up(step, which, own=False):
            return remote(
                index(z - step, y, core), which, me + 2 * y_count, up_sem.at[half, step, which], own
            )

        def to_down(step, which, own=False):
            return remote(
                index(z + step, y, core), which, me - 2 * y_count, down_sem.at[half, step, which], own
            )

        def to_y(z_at, which, own=False):
            return remote(index(z_at, y, core), which, y_peer, y_sem.at[half, z_at, which], own)

        def to_core(z_at, y_at, which, own=False):
            return remote(
                index(z_at, y_at, core), which, sibling, core_sem.at[half, z_at * y_count + y_at, which], own
            )

        def own_copy(which):
            return pltpu.make_async_copy(
                kv_ref.at[which, pl.ds(offset, BLK), pl.ds(half * width, width)], buffer.at[me, which], own_sem.at[half, which]
            )

        def begin():
            for which in range(2):
                pl.when(z < z_count - 1)(lambda: to_up(0, which, True).start())
                pl.when(z > 0)(lambda: to_down(0, which, True).start())
                if y_count > 1:
                    to_y(z, which, True).start()
                to_core(z, y, which, True).start()
            for which in range(2):
                own_copy(which).start()

        def pass_y(distance):
            if y_count == 1:
                return
            for which in range(2):
                def hand(z_at):
                    await_piece(index(z_at, 1 - y, core), which)
                    to_core(z_at, 1 - y, which).start()

                pl.when(z - distance >= 0)(lambda: hand(z - distance))
                if distance:
                    pl.when(z + distance < z_count)(lambda: hand(z + distance))

        def pass_step(step):
            for which in range(2):
                @pl.when(z - step >= 0)
                def _():
                    await_piece(index(z - step, y, core), which)
                    pl.when(z < z_count - 1)(lambda: to_up(step, which).start())
                    if y_count > 1:
                        to_y(z - step, which).start()
                    to_core(z - step, y, which).start()

                @pl.when(z + step < z_count)
                def _():
                    await_piece(index(z + step, y, core), which)
                    pl.when(z > 0)(lambda: to_down(step, which).start())
                    if y_count > 1:
                        to_y(z + step, which).start()
                    to_core(z + step, y, which).start()
            pass_y(step - 1)
        def arrive():
            for which in range(2):
                own_copy(which).wait()
                for z_at in range(z_count):
                    for y_at in range(y_count):
                        await_piece(index(z_at, y_at, 1 - core), which)
        def finish():
            for which in range(2):
                for z_at in range(z_count):
                    if y_count > 1:
                        to_y(z_at, which).wait_send()
                    for y_at in range(y_count):
                        to_core(z_at, y_at, which).wait_send()
                    pl.when((z - z_at >= 0) & (z < z_count - 1))(lambda: to_up(z_at, which).wait_send())
                    pl.when((z + z_at < z_count) & (z > 0))(lambda: to_down(z_at, which).wait_send())


        return begin, pass_step, pass_y, arrive, finish

    def work(low_item, high_item):
        @pl.loop(low_item, high_item)
        def _(item):
            attend_step(
                axis_length, 0, item, frames_ref, sink_ref, q_ref, kv_ref, g_ref, first_ref,
                (out_ref, grad_q_ref, local_ref, entry_ref),
            )

    begin, pass_step, pass_y, arrive, finish = plan(0, first_ref)
    begin_second, pass_step_second, pass_y_second, arrive_second, finish_second = plan(
        1, second_ref
    )
    begin()
    clear_entries(entry_ref, frames_ref.shape[1])
    for step in range(1, z_count):
        pass_step(step)
    begin_second()
    pass_y(z_count - 1)
    arrive()
    done = 0
    for step in range(1, z_count):
        pass_step_second(step)
        upto = min(items, done + step_items)
        if upto > done:
            work(done, upto)
        done = upto
    pass_y_second(z_count - 1)
    assemble(axis_length, frames_ref, sink_ref, entry_ref, parts_ref)
    arrive_second()
    finish()
    finish_second()


def gather_attend(axis_length, y_count, frames, sink, queries, keys_values, cotangent):
    z_count = axis_length // (2 * y_count)
    rows, width = queries.shape
    half = width // 2
    entries = frames.shape[1]
    vmem = pl.BlockSpec(memory_space=pltpu.VMEM)
    smem = pl.BlockSpec(memory_space=pltpu.SMEM)
    hbm = pl.BlockSpec(memory_space=pl.ANY)
    dma = pltpu.SemaphoreType.DMA
    gathered = (axis_length, 2, BLK, half)
    return pl.pallas_call(
        functools.partial(gather_attend_kernel, axis_length, y_count),
        out_shape=(
            jax.ShapeDtypeStruct((rows, half), jnp.bfloat16),
            jax.ShapeDtypeStruct((rows, half), jnp.bfloat16),
            jax.ShapeDtypeStruct((2, rows, half), jnp.float32),
            jax.ShapeDtypeStruct(gathered, jnp.bfloat16),
            jax.ShapeDtypeStruct(gathered, jnp.bfloat16),
        ),
        in_specs=[smem, smem, vmem, vmem, vmem],
        out_specs=[vmem, vmem, vmem, vmem, hbm],
        scratch_shapes=[
            pltpu.VMEM(gathered, jnp.bfloat16),
            pltpu.VMEM((2, entries + 2, 2, BLK, half), jnp.bfloat16),
            dma((2, 2)),
            dma((2, z_count, 2)),
            dma((2, z_count, 2)),
            dma((2, z_count, 2)),
            dma((2, z_count * y_count, 2)),
            dma((2, axis_length, 2)),
        ],
        compiler_params=pltpu.CompilerParams(
            collective_id=0, has_side_effects=True, vmem_limit_bytes=VMEM_BYTES
        ),
        name="gather_attend",
    )(frames, sink, queries, keys_values, cotangent)


def attend_reduce_kernel(
    axis_length,
    y_count,
    frames_ref,
    sink_ref,
    q_ref,
    kv_ref,
    g_ref,
    anchors_ref,
    first_out_ref,
    first_grad_ref,
    first_local_ref,
    first_parts_ref,
    attended_ref,
    grad_q_ref,
    grad_kv_ref,
    second_local_ref,
    second_parts_ref,
    entry_ref,
    from_core,
    from_y,
    from_z,
    core_sum,
    z_term,
    core_send,
    core_recv,
    y_send,
    y_recv,
    z_send,
    z_recv,
):
    z_count = axis_length // (2 * y_count)
    me = lax.axis_index("seq")
    core = me % 2
    y = (me // 2) % y_count
    z = me // (2 * y_count)
    other_y = y_count - 1 - y
    y_peer = (z * y_count + other_y) * 2 + core
    sibling = me + 1 - 2 * core
    offset = core * BLK
    rest = (1 - core) * BLK
    width = anchors_ref.shape[3]
    items = 2 * width // PAIR
    step_items = -(-items // (z_count - 1))
    stride = jnp.where(z < z_count // 2, -1, 1)
    order = [(z + stride * (1 + k) + z_count) % z_count for k in range(z_count)]

    barrier = pltpu.get_barrier_semaphore()
    peers = z_count - 1 + y_count
    for k in range(z_count - 1):
        pl.semaphore_signal(
            barrier, inc=1, device_id={"seq": (order[k] * y_count + y) * 2 + core}
        )
    pl.semaphore_signal(barrier, inc=1, device_id={"seq": sibling})
    if y_count > 1:
        pl.semaphore_signal(barrier, inc=1, device_id={"seq": y_peer})
    pl.semaphore_wait(barrier, peers)

    def plan(half, local_ref, parts_ref):
        def remote(source, place, send_sem, recv_sem, target):
            return pltpu.make_async_remote_copy(
                src_ref=source,
                dst_ref=place,
                send_sem=send_sem,
                recv_sem=recv_sem,
                device_id={"seq": target},
                device_id_type=pl.DeviceIdType.MESH,
            )

        def to_core(piece):
            return remote(
                parts_ref.at[piece * 2 + 1 - core],
                from_core.at[half, piece],
                core_send.at[half, piece],
                core_recv.at[half, piece],
                sibling,
            )

        def to_y(k, which):
            return remote(
                core_sum.at[half, order[k] * y_count + other_y, which],
                from_y.at[half, order[k], which],
                y_send.at[half, k, which],
                y_recv.at[half, k, which],
                y_peer,
            )

        def to_z(k, which):
            return remote(
                z_term.at[half, order[k], which],
                from_z.at[half, z, which],
                z_send.at[half, k, which],
                z_recv.at[half, z, which],
                (order[k] * y_count + y) * 2 + core,
            )

        def from_z_wait(k, which):
            remote(
                z_term.at[half, order[k], which],
                from_z.at[half, order[k], which],
                z_send.at[half, k, which],
                z_recv.at[half, order[k], which],
                sibling,
            ).wait_recv()

        def wide(value):
            return value.astype(jnp.float32)

        def merge_core(piece):
            to_core(piece).wait_recv()
            for which in range(2):
                core_sum[half, piece, which] = (
                    wide(parts_ref[piece * 2 + core, which]) + wide(from_core[half, piece, which])
                ).astype(jnp.bfloat16)

        def begin():
            if y_count > 1:
                for k in range(z_count):
                    to_core(order[k] * y_count + other_y).start()
            for k in range(z_count):
                to_core(order[k] * y_count + y).start()
            if y_count > 1:
                for k in range(z_count):
                    merge_core(order[k] * y_count + other_y)
                    for which in range(2):
                        to_y(k, which).start()
            for k in range(z_count):
                merge_core(order[k] * y_count + y)

        def term_of(k, which):
            term = wide(core_sum[half, order[k] * y_count + y, which])
            if y_count > 1:
                to_y(k, which).wait_recv()
                term = term + wide(from_y[half, order[k], which])
            return term

        def pass_z(k):
            for which in range(2):
                z_term[half, order[k], which] = term_of(k, which).astype(jnp.bfloat16)
                to_z(k, which).start()

        def total():
            cols = pl.ds(half * width, width)
            for which in range(2):
                grad_kv_ref[which, pl.ds(rest, BLK), cols] = local_ref[
                    which, pl.ds(rest, BLK)
                ].astype(jnp.bfloat16)
                summed = term_of(z_count - 1, which) + local_ref[which, pl.ds(offset, BLK)]
                for other in range(z_count - 1):
                    from_z_wait(other, which)
                    summed = summed + wide(from_z[half, order[other], which])
                grad_kv_ref[which, pl.ds(offset, BLK), cols] = summed.astype(jnp.bfloat16)

        def finish():
            for k in range(z_count):
                for y_at in range(y_count):
                    to_core(order[k] * y_count + y_at).wait_send()
                for which in range(2):
                    if y_count > 1:
                        to_y(k, which).wait_send()
                    if k < z_count - 1:
                        to_z(k, which).wait_send()

        return begin, pass_z, total, finish

    def work(low_item, high_item):
        @pl.loop(low_item, high_item)
        def _(item):
            attend_step(
                axis_length, 1, item, frames_ref, sink_ref, q_ref, kv_ref, g_ref, anchors_ref,
                (attended_ref, grad_q_ref, second_local_ref, entry_ref),
            )

    begin, pass_z, total, finish = plan(0, first_local_ref, first_parts_ref)
    begin_second, pass_z_second, total_second, finish_second = plan(
        1, second_local_ref, second_parts_ref
    )
    begin()
    clear_entries(entry_ref, frames_ref.shape[1])
    attended_ref[:, pl.ds(0, width)] = first_out_ref[...]
    grad_q_ref[:, pl.ds(0, width)] = first_grad_ref[...]
    done = 0
    for k in range(z_count - 1):
        upto = min(items, done + step_items)
        if upto > done:
            work(done, upto)
        done = upto
        pass_z(k)
    assemble(axis_length, frames_ref, sink_ref, entry_ref, second_parts_ref)
    begin_second()
    total()
    for k in range(z_count - 1):
        pass_z_second(k)
    total_second()
    finish()
    finish_second()


def attend_reduce(axis_length, y_count, frames, sink, queries, keys_values, cotangent, gathered):
    attended, grad_queries, local, parts, anchors = gathered
    z_count = axis_length // (2 * y_count)
    chips = axis_length // 2
    tile = parts.shape[1:]
    entries = frames.shape[1]
    vmem = pl.BlockSpec(memory_space=pltpu.VMEM)
    smem = pl.BlockSpec(memory_space=pltpu.SMEM)
    dma = pltpu.SemaphoreType.DMA
    return pl.pallas_call(
        functools.partial(attend_reduce_kernel, axis_length, y_count),
        out_shape=(
            jax.ShapeDtypeStruct(queries.shape, jnp.bfloat16),
            jax.ShapeDtypeStruct(queries.shape, jnp.bfloat16),
            jax.ShapeDtypeStruct(keys_values.shape, jnp.bfloat16),
        ),
        in_specs=[smem, smem] + [vmem] * 8,
        out_specs=[vmem] * 3,
        scratch_shapes=[
            pltpu.VMEM(local.shape, jnp.float32),
            pltpu.VMEM(parts.shape, jnp.bfloat16),
            pltpu.VMEM((2, entries + 2) + tile, jnp.bfloat16),
            pltpu.VMEM((2, chips) + tile, jnp.bfloat16),
            pltpu.VMEM((2, z_count) + tile, jnp.bfloat16),
            pltpu.VMEM((2, z_count) + tile, jnp.bfloat16),
            pltpu.VMEM((2, chips) + tile, jnp.bfloat16),
            pltpu.VMEM((2, z_count) + tile, jnp.bfloat16),
            dma((2, chips)),
            dma((2, chips)),
            dma((2, z_count, 2)),
            dma((2, z_count, 2)),
            dma((2, z_count, 2)),
            dma((2, z_count, 2)),
        ],
        compiler_params=pltpu.CompilerParams(
            collective_id=1, has_side_effects=True, vmem_limit_bytes=VMEM_BYTES
        ),
        name="attend_reduce",
    )(
        frames, sink, queries, keys_values, cotangent, anchors,
        attended, grad_queries, local, parts,
    )


def shards(y_count, queries, keys_values, cotangent, frame_lists, sink_owner):
    axis_length = lax.axis_size("seq")
    args = (axis_length, y_count, frame_lists, sink_owner, queries, keys_values, cotangent)
    return attend_reduce(*args, gather_attend(*args))


def solution(mesh):
    rows = P(("groups", "seq"), None)
    pairs = P(None, ("groups", "seq"), None)
    y_count = 2 if mesh.shape["groups"] == 2 and mesh.shape["seq"] % 4 == 0 else 1
    return jax.shard_map(
        functools.partial(shards, y_count),
        mesh=mesh,
        in_specs=(rows, pairs, rows, rows, P("groups")),
        out_specs=(rows, rows, pairs),
        check_vma=False,
    )
```

time: 194 us -> 107 us (0.55)
  the two profiles are of different devices: /device:TPU:11 before, /device:TPU:0 now
where the time goes in v3:
time: 107 us; the launch traced here: 106 us
  Pallas kernels  99.4 us (93%)
  local copies, waits for them, and re-layouts  5.6 us (5%)
  between operations  1.29 us (1%)
    pallas_call x1, Pallas kernels, attend_reduce(): pl.pallas_call(functools.partial(attend_reduce_kernel, axis_length, y_cou...  50.8 us
    pallas_call x1, Pallas kernels, gather_attend(): pl.pallas_call(functools.partial(gather_attend_kernel, axis_length, y_cou...  48.6 us
    unnamed x3, local copies, waits for them, and re-layouts  5.6 us

profile of v3, /device:TPU:0, one launch (start us, length us, event | category | flops | bytes accessed | tf_op | source)
XLA Modules:
  0.0 106.3 jit_solution(14084089648337990478)
XLA Ops:
  1.3 48.6 %gather_attend.1 = (bf16[256,384]{1,0:T(8,128)(2,1)}, bf16[256,384]{1,0:T(8,128)(2,1)}, f32[2,256,384]{2,1,0:T(8,128)}, bf16[16,2,128,384]{3,2,1,0:T(8,128)(2,1)}, bf16[16,2,128,384]{3,2,1,0:T(8,128)(2,1)}) custom-call(s32[2,6]{1,0:T(2,128)} %frames_ref.3, s32[1]{0:T(128)S(6)} %copy.11.sink_ref, bf16[256,768]{1,0:T(8,128)(2,1)} %q_ref.3, ...), custom_call_target="tpu_custom_call" | custom-call | tf_op jit(solution)/shard_map/gather_attend/pallas_call | solution.py:327
  49.9 50.8 %attend_reduce.1 = (bf16[256,768]{1,0:T(8,128)(2,1)}, bf16[256,768]{1,0:T(8,128)(2,1)}, bf16[2,256,768]{2,1,0:T(8,128)(2,1)}) custom-call(s32[2,6]{1,0:T(2,128)} %frames_ref.3, s32[1]{0:T(128)S(6)} %copy.11.sink_ref, bf16[256,768]{1,0:T(8,128)(2,1)} %q_ref.3, bf16[2,256,768]{2,1,0:T(8,128)(2,1)} %kv_ref.3, bf16[256,768]{1,0:T(8,128)(2,1)} %g_ref.3, ...), custom_call_target="tpu_custom_call" | custom-call | tf_op jit(solution)/shard_map/attend_reduce/pallas_call | solution.py:562
  100.7 1.8 %copy.12 = bf16[256,768]{1,0:T(8,128)(2,1)} copy(bf16[256,768]{1,0:T(8,128)(2,1)} %get-tuple-element.16) | data formatting | bytes 786432
  102.5 1.8 %copy.13 = bf16[256,768]{1,0:T(8,128)(2,1)} copy(bf16[256,768]{1,0:T(8,128)(2,1)} %get-tuple-element.17) | data formatting | bytes 786432
  104.2 2.1 %copy.14 = bf16[2,256,768]{2,1,0:T(8,128)(2,1)} copy(bf16[2,256,768]{2,1,0:T(8,128)(2,1)} %get-tuple-element.18) | data formatting | bytes 1572864

commit v4 on v3

--- a/solution.py
+++ b/solution.py
@@ -138,16 +138,21 @@
     y_count,
     frames_ref,
     sink_ref,
+    q_hbm,
+    kv_hbm,
+    g_hbm,
+    out_ref,
+    grad_q_ref,
+    local_ref,
+    parts_hbm,
+    second_ref,
+    first_ref,
+    entry_ref,
     q_ref,
     kv_ref,
     g_ref,
-    out_ref,
-    grad_q_ref,
-    local_ref,
     parts_ref,
-    second_ref,
-    first_ref,
-    entry_ref,
+    load_sem,
     own_sem,
     up_sem,
     down_sem,
@@ -186,7 +191,7 @@
     def plan(half, buffer):
         def remote(piece, which, target, send_sem, own=False):
             place = buffer.at[piece, which]
-            source = kv_ref.at[which, pl.ds(offset, BLK), pl.ds(half * width, width)] if own else place
+            source = kv_hbm.at[which, pl.ds(offset, BLK), pl.ds(half * width, width)] if own else place
             return pltpu.make_async_remote_copy(
                 src_ref=source,
                 dst_ref=place,
@@ -219,7 +224,7 @@
 
         def own_copy(which):
             return pltpu.make_async_copy(
-                kv_ref.at[which, pl.ds(offset, BLK), pl.ds(half * width, width)], buffer.at[me, which], own_sem.at[half, which]
+                kv_hbm.at[which, pl.ds(offset, BLK), pl.ds(half * width, width)], buffer.at[me, which], own_sem.at[half, which]
             )
 
         def begin():
@@ -293,13 +298,21 @@
     begin_second, pass_step_second, pass_y_second, arrive_second, finish_second = plan(
         1, second_ref
     )
+    loads = [
+        pltpu.make_async_copy(source, place, load_sem.at[k])
+        for k, (source, place) in enumerate(((q_hbm, q_ref), (kv_hbm, kv_ref), (g_hbm, g_ref)))
+    ]
     begin()
+    for load in loads:
+        load.start()
     clear_entries(entry_ref, frames_ref.shape[1])
     for step in range(1, z_count):
         pass_step(step)
     begin_second()
     pass_y(z_count - 1)
     arrive()
+    for load in loads:
+        load.wait()
     done = 0
     for step in range(1, z_count):
         pass_step_second(step)
@@ -309,9 +322,12 @@
         done = upto
     pass_y_second(z_count - 1)
     assemble(axis_length, frames_ref, sink_ref, entry_ref, parts_ref)
+    store = pltpu.make_async_copy(parts_ref, parts_hbm, load_sem.at[3])
+    store.start()
     arrive_second()
     finish()
     finish_second()
+    store.wait()
 
 
 def gather_attend(axis_length, y_count, frames, sink, queries, keys_values, cotangent):
@@ -333,11 +349,16 @@
             jax.ShapeDtypeStruct(gathered, jnp.bfloat16),
             jax.ShapeDtypeStruct(gathered, jnp.bfloat16),
         ),
-        in_specs=[smem, smem, vmem, vmem, vmem],
-        out_specs=[vmem, vmem, vmem, vmem, hbm],
+        in_specs=[smem, smem, hbm, hbm, hbm],
+        out_specs=[vmem, vmem, vmem, hbm, hbm],
         scratch_shapes=[
             pltpu.VMEM(gathered, jnp.bfloat16),
             pltpu.VMEM((2, entries + 2, 2, BLK, half), jnp.bfloat16),
+            pltpu.VMEM(queries.shape, jnp.bfloat16),
+            pltpu.VMEM(keys_values.shape, jnp.bfloat16),
+            pltpu.VMEM(cotangent.shape, jnp.bfloat16),
+            pltpu.VMEM(gathered, jnp.bfloat16),
+            dma((4,)),
             dma((2, 2)),
             dma((2, z_count, 2)),
             dma((2, z_count, 2)),
@@ -357,20 +378,27 @@
     y_count,
     frames_ref,
     sink_ref,
-    q_ref,
-    kv_ref,
-    g_ref,
-    anchors_ref,
+    q_hbm,
+    kv_hbm,
+    g_hbm,
+    anchors_hbm,
     first_out_ref,
     first_grad_ref,
-    first_local_ref,
-    first_parts_ref,
+    first_local_hbm,
+    first_parts_hbm,
     attended_ref,
     grad_q_ref,
     grad_kv_ref,
     second_local_ref,
     second_parts_ref,
     entry_ref,
+    q_ref,
+    kv_ref,
+    g_ref,
+    anchors_ref,
+    first_local_ref,
+    first_parts_ref,
+    load_sem,
     from_core,
     from_y,
     from_z,
@@ -399,6 +427,20 @@
     stride = jnp.where(z < z_count // 2, -1, 1)
     order = [(z + stride * (1 + k) + z_count) % z_count for k in range(z_count)]
 
+    pairs_of_refs = (
+        (first_parts_hbm, first_parts_ref),
+        (anchors_hbm, anchors_ref),
+        (q_hbm, q_ref),
+        (kv_hbm, kv_ref),
+        (g_hbm, g_ref),
+        (first_local_hbm, first_local_ref),
+    )
+    loads = [
+        pltpu.make_async_copy(source, place, load_sem.at[k])
+        for k, (source, place) in enumerate(pairs_of_refs)
+    ]
+    for load in loads:
+        load.start()
     barrier = pltpu.get_barrier_semaphore()
     peers = z_count - 1 + y_count
     for k in range(z_count - 1):
@@ -410,7 +452,7 @@
         pl.semaphore_signal(barrier, inc=1, device_id={"seq": y_peer})
     pl.semaphore_wait(barrier, peers)
 
-    def plan(half, local_ref, parts_ref):
+    def plan(half, local_ref, parts_ref, send_ref):
         def remote(source, place, send_sem, recv_sem, target):
             return pltpu.make_async_remote_copy(
                 src_ref=source,
@@ -423,7 +465,7 @@
 
         def to_core(piece):
             return remote(
-                parts_ref.at[piece * 2 + 1 - core],
+                send_ref.at[piece * 2 + 1 - core],
                 from_core.at[half, piece],
                 core_send.at[half, piece],
                 core_recv.at[half, piece],
@@ -473,6 +515,8 @@
                     to_core(order[k] * y_count + other_y).start()
             for k in range(z_count):
                 to_core(order[k] * y_count + y).start()
+
+        def merge():
             if y_count > 1:
                 for k in range(z_count):
                     merge_core(order[k] * y_count + other_y)
@@ -515,7 +559,7 @@
                     if k < z_count - 1:
                         to_z(k, which).wait_send()
 
-        return begin, pass_z, total, finish
+        return begin, merge, pass_z, total, finish
 
     def work(low_item, high_item):
         @pl.loop(low_item, high_item)
@@ -525,14 +569,20 @@
                 (attended_ref, grad_q_ref, second_local_ref, entry_ref),
             )
 
-    begin, pass_z, total, finish = plan(0, first_local_ref, first_parts_ref)
-    begin_second, pass_z_second, total_second, finish_second = plan(
-        1, second_local_ref, second_parts_ref
+    begin, merge, pass_z, total, finish = plan(
+        0, first_local_ref, first_parts_ref, first_parts_hbm
+    )
+    begin_second, merge_second, pass_z_second, total_second, finish_second = plan(
+        1, second_local_ref, second_parts_ref, second_parts_ref
     )
     begin()
+    loads[0].wait()
+    merge()
     clear_entries(entry_ref, frames_ref.shape[1])
     attended_ref[:, pl.ds(0, width)] = first_out_ref[...]
     grad_q_ref[:, pl.ds(0, width)] = first_grad_ref[...]
+    for load in loads[1:]:
+        load.wait()
     done = 0
     for k in range(z_count - 1):
         upto = min(items, done + step_items)
@@ -542,8 +592,10 @@
         pass_z(k)
     assemble(axis_length, frames_ref, sink_ref, entry_ref, second_parts_ref)
     begin_second()
-    total()
+    merge_second()
     for k in range(z_count - 1):
+        if k == z_count // 2:
+            total()
         pass_z_second(k)
     total_second()
     finish()
@@ -558,6 +610,7 @@
     entries = frames.shape[1]
     vmem = pl.BlockSpec(memory_space=pltpu.VMEM)
     smem = pl.BlockSpec(memory_space=pltpu.SMEM)
+    hbm = pl.BlockSpec(memory_space=pl.ANY)
     dma = pltpu.SemaphoreType.DMA
     return pl.pallas_call(
         functools.partial(attend_reduce_kernel, axis_length, y_count),
@@ -566,14 +619,21 @@
             jax.ShapeDtypeStruct(queries.shape, jnp.bfloat16),
             jax.ShapeDtypeStruct(keys_values.shape, jnp.bfloat16),
         ),
-        in_specs=[smem, smem] + [vmem] * 8,
+        in_specs=[smem, smem] + [hbm] * 4 + [vmem] * 2 + [hbm] * 2,
         out_specs=[vmem] * 3,
         scratch_shapes=[
             pltpu.VMEM(local.shape, jnp.float32),
             pltpu.VMEM(parts.shape, jnp.bfloat16),
             pltpu.VMEM((2, entries + 2) + tile, jnp.bfloat16),
+            pltpu.VMEM(queries.shape, jnp.bfloat16),
+            pltpu.VMEM(keys_values.shape, jnp.bfloat16),
+            pltpu.VMEM(cotangent.shape, jnp.bfloat16),
+            pltpu.VMEM(anchors.shape, jnp.bfloat16),
+            pltpu.VMEM(local.shape, jnp.float32),
+            pltpu.VMEM(parts.shape, jnp.bfloat16),
+            dma((6,)),
             pltpu.VMEM((2, chips) + tile, jnp.bfloat16),
-            pltpu.VMEM((2, z_count) + tile, jnp.bfloat16),
+            pltpu.VMEM((2, z_count if y_count > 1 else 1) + tile, jnp.bfloat16),
             pltpu.VMEM((2, z_count) + tile, jnp.bfloat16),
             pltpu.VMEM((2, chips) + tile, jnp.bfloat16),
             pltpu.VMEM((2, z_count) + tile, jnp.bfloat16),
@@ -594,10 +654,42 @@
     )
 
 
+def publish_kernel(*refs):
+    sources, places, sem = refs[:3], refs[3:6], refs[6]
+    copies = []
+    for source, place in zip(sources, places):
+        rows = source.shape[0] // 4
+        for part in range(4):
+            here = pl.ds(part * rows, rows)
+            copies.append(
+                pltpu.make_async_copy(source.at[here], place.at[here], sem.at[len(copies)])
+            )
+    for copy in copies:
+        copy.start()
+    for copy in copies:
+        copy.wait()
+
+
+def publish(attended, grad_queries, grad_keys_values):
+    hbm = pl.BlockSpec(memory_space=pl.ANY)
+    shape = grad_keys_values.shape
+    flat = grad_keys_values.reshape(shape[0] * shape[1], shape[2])
+    arrays = (attended, grad_queries, flat)
+    outs = pl.pallas_call(
+        publish_kernel,
+        out_shape=tuple(jax.ShapeDtypeStruct(a.shape, a.dtype) for a in arrays),
+        in_specs=[hbm] * 3,
+        out_specs=[hbm] * 3,
+        scratch_shapes=[pltpu.SemaphoreType.DMA((12,))],
+        name="publish",
+    )(*arrays)
+    return outs[0], outs[1], outs[2].reshape(shape)
+
+
 def shards(y_count, queries, keys_values, cotangent, frame_lists, sink_owner):
     axis_length = lax.axis_size("seq")
     args = (axis_length, y_count, frame_lists, sink_owner, queries, keys_values, cotangent)
-    return attend_reduce(*args, gather_attend(*args))
+    return publish(*attend_reduce(*args, gather_attend(*args)))
 
 
 def solution(mesh):

time: 107 us -> 145 us (1.36)
  the two profiles are of different devices: /device:TPU:0 before, /device:TPU:11 now
where the time goes in v4:
time: 145 us
  Pallas kernels  143 us (99%)
    pallas_call x1, Pallas kernels, publish(): pl.pallas_call(publish_kernel, out_shape=tuple((jax.ShapeDtypeStruct(a.sh...  48.9 us
    pallas_call x1, Pallas kernels, attend_reduce(): pl.pallas_call(functools.partial(attend_reduce_kernel, axis_length, y_cou...  48.3 us
    pallas_call x1, Pallas kernels, gather_attend(): pl.pallas_call(functools.partial(gather_attend_kernel, axis_length, y_cou...  46.2 us

profile of v4, /device:TPU:11, one launch (start us, length us, event | category | flops | bytes accessed | tf_op | source)
XLA Modules:
  0.0 144.6 jit_solution(10975885154080014158)
XLA Ops:
  1.3 46.2 %gather_attend.1 = (bf16[256,384]{1,0:T(8,128)(2,1)}, bf16[256,384]{1,0:T(8,128)(2,1)}, f32[2,256,384]{2,1,0:T(8,128)}, bf16[16,2,128,384]{3,2,1,0:T(8,128)(2,1)}, bf16[16,2,128,384]{3,2,1,0:T(8,128)(2,1)}) custom-call(s32[2,6]{1,0:T(2,128)} %frames_ref.3, s32[1]{0:T(128)S(6)} %copy.8.sink_ref, bf16[256,768]{1,0:T(8,128)(2,1)} %q_hbm.3, ...), custom_call_target="tpu_custom_call" | custom-call | tf_op jit(solution)/shard_map/gather_attend/pallas_call | solution.py:343
  47.5 48.3 %attend_reduce.1 = (bf16[256,768]{1,0:T(8,128)(2,1)}, bf16[256,768]{1,0:T(8,128)(2,1)}, bf16[2,256,768]{2,1,0:T(8,128)(2,1)}) custom-call(s32[2,6]{1,0:T(2,128)} %frames_ref.3, s32[1]{0:T(128)S(6)} %copy.8.sink_ref, bf16[256,768]{1,0:T(8,128)(2,1)} %q_hbm.3, bf16[2,256,768]{2,1,0:T(8,128)(2,1)} %kv_hbm.3, bf16[256,768]{1,0:T(8,128)(2,1)} %g_hbm.3, ...), custom_call_target="tpu_custom_call" | custom-call | tf_op jit(solution)/shard_map/attend_reduce/pallas_call | solution.py:615
  95.8 48.9 %publish.1 = (bf16[256,768]{1,0:T(8,128)(2,1)}, bf16[256,768]{1,0:T(8,128)(2,1)}, bf16[512,768]{1,0:T(8,128)(2,1)}) custom-call(bf16[256,768]{1,0:T(8,128)(2,1)} %get-tuple-element.19.refs_0_, bf16[256,768]{1,0:T(8,128)(2,1)} %get-tuple-element.20.refs_1_, bf16[512,768]{1,0:T(8,128)(2,1)} %bitcast.2), custom_call_target="tpu_custom_call" | custom-call | tf_op jit(solution)/shard_map/publish/pallas_call | solution.py:678

commit v5 on v4

--- a/solution.py
+++ b/solution.py
@@ -655,19 +655,26 @@
 
 
 def publish_kernel(*refs):
-    sources, places, sem = refs[:3], refs[3:6], refs[6]
-    copies = []
-    for source, place in zip(sources, places):
+    sources, places, holds, load_sem, store_sem = refs[:3], refs[3:6], refs[6:9], refs[9], refs[10]
+    loads, stores = [], []
+    for source, place, hold in zip(sources, places, holds):
         rows = source.shape[0] // 4
         for part in range(4):
             here = pl.ds(part * rows, rows)
-            copies.append(
-                pltpu.make_async_copy(source.at[here], place.at[here], sem.at[len(copies)])
-            )
-    for copy in copies:
-        copy.start()
-    for copy in copies:
-        copy.wait()
+            k = len(loads)
+            loads.append(
+                pltpu.make_async_copy(source.at[here], hold.at[here], load_sem.at[k])
+            )
+            stores.append(
+                pltpu.make_async_copy(hold.at[here], place.at[here], store_sem.at[k])
+            )
+    for load in loads:
+        load.start()
+    for load, store in zip(loads, stores):
+        load.wait()
+        store.start()
+    for store in stores:
+        store.wait()
 
 
 def publish(attended, grad_queries, grad_keys_values):
@@ -680,7 +687,8 @@
         out_shape=tuple(jax.ShapeDtypeStruct(a.shape, a.dtype) for a in arrays),
         in_specs=[hbm] * 3,
         out_specs=[hbm] * 3,
-        scratch_shapes=[pltpu.SemaphoreType.DMA((12,))],
+        scratch_shapes=[pltpu.VMEM(a.shape, a.dtype) for a in arrays]
+        + [pltpu.SemaphoreType.DMA((12,)), pltpu.SemaphoreType.DMA((12,))],
         name="publish",
     )(*arrays)
     return outs[0], outs[1], outs[2].reshape(shape)

time: 145 us -> 98.3 us (0.68)
  Pallas kernels: 143 us -> 96.9 us
    pallas_call x1, Pallas kernels: 48.9 us -> 2.36 us  [publish(): pl.pallas_call(publish_kernel, out_shape=tuple((jax.ShapeDtypeStruct(a.sh...]
where the time goes in v5:
time: 98.3 us; the launch traced here: 98.1 us
  Pallas kernels  96.9 us (99%)
  between operations  1.29 us (1%)
    pallas_call x1, Pallas kernels, attend_reduce(): pl.pallas_call(functools.partial(attend_reduce_kernel, axis_length, y_cou...  48.3 us
    pallas_call x1, Pallas kernels, gather_attend(): pl.pallas_call(functools.partial(gather_attend_kernel, axis_length, y_cou...  46.2 us
    pallas_call x1, Pallas kernels, publish(): pl.pallas_call(publish_kernel, out_shape=tuple((jax.ShapeDtypeStruct(a.sh...  2.36 us

profile of v5, /device:TPU:11, one launch (start us, length us, event | category | flops | bytes accessed | tf_op | source)
XLA Modules:
  0.0 98.1 jit_solution(10300329991774773689)
XLA Ops:
  1.3 46.2 %gather_attend.1 = (bf16[256,384]{1,0:T(8,128)(2,1)}, bf16[256,384]{1,0:T(8,128)(2,1)}, f32[2,256,384]{2,1,0:T(8,128)}, bf16[16,2,128,384]{3,2,1,0:T(8,128)(2,1)}, bf16[16,2,128,384]{3,2,1,0:T(8,128)(2,1)}) custom-call(s32[2,6]{1,0:T(2,128)} %frames_ref.3, s32[1]{0:T(128)S(6)} %copy.8.sink_ref, bf16[256,768]{1,0:T(8,128)(2,1)} %q_hbm.3, ...), custom_call_target="tpu_custom_call" | custom-call | tf_op jit(solution)/shard_map/gather_attend/pallas_call | solution.py:343
  47.5 48.3 %attend_reduce.1 = (bf16[256,768]{1,0:T(8,128)(2,1)}, bf16[256,768]{1,0:T(8,128)(2,1)}, bf16[2,256,768]{2,1,0:T(8,128)(2,1)}) custom-call(s32[2,6]{1,0:T(2,128)} %frames_ref.3, s32[1]{0:T(128)S(6)} %copy.8.sink_ref, bf16[256,768]{1,0:T(8,128)(2,1)} %q_hbm.3, bf16[2,256,768]{2,1,0:T(8,128)(2,1)} %kv_hbm.3, bf16[256,768]{1,0:T(8,128)(2,1)} %g_hbm.3, ...), custom_call_target="tpu_custom_call" | custom-call | tf_op jit(solution)/shard_map/attend_reduce/pallas_call | solution.py:615
  95.8 2.4 %publish.1 = (bf16[256,768]{1,0:T(8,128)(2,1)}, bf16[256,768]{1,0:T(8,128)(2,1)}, bf16[512,768]{1,0:T(8,128)(2,1)}) custom-call(bf16[256,768]{1,0:T(8,128)(2,1)} %get-tuple-element.19.refs_0_, bf16[256,768]{1,0:T(8,128)(2,1)} %get-tuple-element.20.refs_1_, bf16[512,768]{1,0:T(8,128)(2,1)} %bitcast.2), custom_call_target="tpu_custom_call" | custom-call | tf_op jit(solution)/shard_map/publish/pallas_call | solution.py:685
